TPU v7x, 768 devices: a whole 4x8x12 slice. The times are simulated.
768 devices in a mesh: gz: 96 (over y, z), ta: 8 (over x, core).
Axes of the slice: x: 4, y: 8, z: 12, core: 2. Of those that a mesh axis runs over, the one named last changes fastest.
Arguments:
- log_mean: float32 [96, 512, 512], P('gz', 'ta'), may hold values from -6 to 6
- tile_mask: int32 [96, 512, 512], P('gz', 'ta'), may hold values 0 or 1
- coverage: int32 [96, 512, 512], P('gz', 'ta'), may hold values from 0 to 4096
- lifetime: float32 [512, 512], P('ta'), may hold values from 0 to 40, as said below
- keep: float32 [96], replicated, may hold values from 0 to 1, as said below
Outputs:
- corrected: float32 [96, 512, 512], P('gz', None, 'ta')
Inputs may be any that keep to these rules, and one draw needn't show every extreme that they name: `lifetime`: positive. `keep`: positive.
All inputs are finite; a program needn't handle non-finite values. No bound on the sum of `tile_mask` on one device may be relied on, other than what follows from the above.
Results may differ from a plain program's by a relative error of at most 0.0003.
Values sent between devices are 32-bit elements; how exact they have to be, the bound alone decides.
No kernel may reach another device: no remote copies, remote signals or barrier semaphores. Data moves between devices by JAX's collectives and lax.ppermute only.
A program may use at most 128 MiB of HBM per device.

v0:
```python
import jax
import jax.numpy as jnp
from jax import lax
from jax.sharding import PartitionSpec as P

RADIUS = 8
PASSES = 7


def padded(shard, sides, width):
    for axis, dim in sides:
        size, length = (lax.axis_size(axis), shard.shape[dim])
        up = [(i, (i + 1) % size) for i in range(size - 1)]
        down = [(j, i) for i, j in up]
        last = lax.slice_in_dim(shard, length - width, length, axis=dim)
        initial = lax.slice_in_dim(shard, 0, width, axis=dim)
        before = lax.ppermute(last, axis, up)
        after = lax.ppermute(initial, axis, down)
        shard = jnp.concatenate([before, shard, after], axis=dim)
    return shard


def carried_in(part, axis, combine, identity, reverse):
    count = lax.axis_size(axis)
    place = lax.axis_index(axis)
    ahead = count - 1 - place if reverse else place
    gathered = jax.tree.map(lambda a: lax.all_gather(a, axis), part)
    state = jax.tree.map(lambda a, e: jnp.zeros_like(a) + jnp.asarray(e, a.dtype), part, identity)

    def one(lap, state):
        source = count - 1 - lap if reverse else lap
        return combine(
            state, jax.tree.map(lambda a: lax.dynamic_index_in_dim(a, source, 0, False), gathered)
        )

    return lax.fori_loop(0, ahead, one, state)


def column_band(width_count, radius):
    places = jnp.arange(width_count)
    return (jnp.abs(places[:, None] - places[None, :]) <= radius).astype(jnp.float32)


def box_columns(values, radius):
    band = column_band(values.shape[-1], radius)
    return jnp.einsum("srw,wv->srv", values, band, precision=lax.Precision.HIGHEST)


def box_inner(values, radius):
    rows_in = values.shape[1]
    rows_out = rows_in - 2 * radius
    outer = jnp.arange(rows_out)[:, None]
    inner = jnp.arange(rows_in)[None, :]
    offset = inner - outer
    band = ((offset >= 0) & (offset <= 2 * radius)).astype(jnp.float32)
    return jnp.einsum("oi,siw->sow", band, values, precision=lax.Precision.HIGHEST)


def affine_join(earlier, latter):
    return (
        earlier[0] * latter[0],
        latter[0] * earlier[1] + latter[1],
        latter[0] * earlier[2] + latter[2],
    )


def shards(log_mean, tile_mask, coverage, lifetime, keep):
    sec_count = log_mean.shape[0]
    total_sections = keep.shape[0]
    weight = 1.0 + tile_mask.astype(jnp.float32) * coverage.astype(jnp.float32)
    weight_wide = padded(box_columns(weight, RADIUS), (("ta", 1),), RADIUS)
    denom = box_inner(weight_wide, RADIUS)
    field_now = log_mean
    for level in range(PASSES):
        rim_field = padded(box_columns(weight * field_now, RADIUS), (("ta", 1),), RADIUS)
        field_now = box_inner(rim_field, RADIUS) / denom
    rate = lifetime / total_sections
    fade = jnp.exp(-rate)
    first = lax.axis_index("gz") * sec_count
    keep_local = lax.dynamic_slice_in_dim(keep, first, sec_count)
    decay = keep_local[:, None, None] * fade[None]
    gain = 1.0 - decay
    zero_field = jnp.zeros(lifetime.shape, jnp.float32)
    unit_field = jnp.ones(lifetime.shape, jnp.float32)
    product, mass, norm_sum = (unit_field, zero_field, zero_field)
    section = 0
    mass = decay[section] * mass + gain[section] * field_now[section]
    norm_sum = decay[section] * norm_sum + gain[section]
    product = decay[section] * product
    arriving_section = carried_in(
        (product, mass, norm_sum), "gz", affine_join, (unit_field, zero_field, zero_field), False
    )
    mass, norm_sum = (arriving_section[1], arriving_section[2])
    section = 0
    mass = decay[section] * mass + gain[section] * field_now[section]
    norm_sum = decay[section] * norm_sum + gain[section]
    forward_list = [mass / norm_sum]
    product, mass, norm_sum = (unit_field, zero_field, zero_field)
    for section in reversed(range(sec_count)):
        mass = decay[section] * mass + gain[section] * forward_list[section]
        norm_sum = decay[section] * norm_sum + gain[section]
        product = decay[section] * product
    arriving_section = carried_in(
        (product, mass, norm_sum), "gz", affine_join, (unit_field, zero_field, zero_field), True
    )
    mass, norm_sum = (arriving_section[1], arriving_section[2])
    drift_values = [zero_field] * sec_count
    for section in reversed(range(sec_count)):
        mass = decay[section] * mass + gain[section] * forward_list[section]
        norm_sum = decay[section] * norm_sum + gain[section]
        drift_values[section] = mass / norm_sum
    drift = jnp.stack(drift_values)
    corrected = log_mean - field_now + drift
    return lax.all_to_all(corrected, "ta", split_axis=2, concat_axis=1, tiled=True)


def solution(mesh):
    return jax.shard_map(
        shards,
        mesh=mesh,
        in_specs=(
            P("gz", "ta", None),
            P("gz", "ta", None),
            P("gz", "ta", None),
            P("ta", None),
            P(),
        ),
        out_specs=P("gz", None, "ta"),
        check_vma=False,
    )
```

profile of v0, /device:TPU:1, one launch (start us, length us, event | category | flops | bytes accessed | tf_op | source)
XLA Modules:
  0.0 866.6 jit_solution(13599283222480915465)
XLA Ops:
  6.5 1.2 dynamic_slice.38
  7.8 2.2 subtract_add_fusion
  12.1 4.5 collective-permute-start.2
  16.7 9.2 %collective-permute-start.3 = (f32[1,8,512]{2,1,0:T(8,128)S(1)}, f32[1,8,512]{2,1,0:T(8,128)S(1)}, u32[]{:S(2)}, u32[]{:S(2)}) collective-permute-start(f32[1,8,512]{2,1,0:T(8,128)S(1)} %get-tuple-element.230), channel_id=1, source_target_pairs={{1,0},{2,1},{3,2},{4,3},{5,4},{6,5},{7,6},{9,8},{10,9},{11,10},{12... | collective-permute-start | bytes 49160 | tf_op jit(solution)/shard_map/ppermute | solution.py:18
  25.8 1.2 convolution_bitcast_fusion.7
  27.1 1.9 collective-permute-start
  29.0 2.4 collective-permute-start.1
  31.7 2.4 collective-permute-done.1
  34.7 1.9 collective-permute-start.4
  36.6 2.4 collective-permute-start.5
  39.0 3.0 collective-permute-done.5
  42.7 1.9 collective-permute-start.6
  44.6 2.4 collective-permute-start.7
  47.0 3.0 collective-permute-done.7
  50.7 1.9 collective-permute-start.8
  52.6 2.4 collective-permute-start.9
  55.0 3.0 collective-permute-done.9
  58.6 1.9 collective-permute-start.10
  60.5 2.4 collective-permute-start.11
  63.0 3.0 collective-permute-done.11
  66.6 1.9 collective-permute-start.12
  68.5 2.4 collective-permute-start.13
  70.9 3.0 collective-permute-done.13
  74.6 1.9 collective-permute-start.14
  76.5 2.4 collective-permute-start.15
  78.9 2.6 collective-permute-done.15
  81.5 1.8 fusion.54
  83.4 86.2 %all-gather.10.cloned.1.call-done = f32[6144,512]{1,0:T(8,128)} async-done(((f32[64,512]{1,0:T(8,128)}), f32[6144,512]{1,0:T(8,128)}) %all-gather.10.cloned.1.call-update) | async-done | bytes 12582928 | tf_op jit(solution)/shard_map/all_gather | solution.py:27
  169.6 153.3 %all-gather.12.cloned.1.call-done = f32[6144,512]{1,0:T(8,128)} async-done(((f32[64,512]{1,0:T(8,128)}), f32[6144,512]{1,0:T(8,128)}) %all-gather.12.cloned.1.call-update) | async-done | bytes 12582928 | tf_op jit(solution)/shard_map/all_gather | solution.py:27
  322.9 153.3 %all-gather.8.cloned.1.call-done = f32[96,64,512]{2,1,0:T(8,128)} async-done(((f32[1,64,512]{2,1,0:T(8,128)}), f32[96,64,512]{2,1,0:T(8,128)}) %all-gather.8.cloned.1.call-update) | async-done | bytes 12582928 | tf_op jit(solution)/shard_map/all_gather | solution.py:27
  477.0 255.0 %all-gather.14.cloned.1.call-done = f32[6144,512]{1,0:T(8,128)} async-done(((f32[64,512]{1,0:T(8,128)}), f32[6144,512]{1,0:T(8,128)}) %all-gather.14.cloned.1.call-update) | async-done | bytes 12582928 | tf_op jit(solution)/shard_map/all_gather | solution.py:27
  732.1 110.9 %while.31 = (s32[]{:T(128)}, f32[64,512]{1,0:T(8,128)S(1)}, f32[64,512]{1,0:T(8,128)S(1)}, s32[]{:T(128)}, f32[96,64,512]{2,1,0:T(8,128)}, /*index=5*/f32[96,64,...) while((s32[]{:T(128)}, f32[64,512]{1,0:T(8,128)S(1)}, ...), condition=%wide.region_3.4_spmd, body=%wide.region_2.3_spmd.sunk | while | flops 131078 | bytes 917663 | solution.py:36
  733.3 1.1 bitcast_add_fusion.8
  734.4 1.1 bitcast_add_fusion.8
  735.6 1.1 bitcast_add_fusion.8
  736.8 1.1 bitcast_add_fusion.8
  737.9 1.1 bitcast_add_fusion.8
  739.1 1.1 bitcast_add_fusion.8
  744.9 1.1 bitcast_add_fusion.8
  746.1 1.1 bitcast_add_fusion.8
  747.3 1.1 bitcast_add_fusion.8
  748.4 1.1 bitcast_add_fusion.8
  749.6 1.1 bitcast_add_fusion.8
  750.8 1.1 bitcast_add_fusion.8
  755.4 1.1 bitcast_add_fusion.8
  756.6 1.1 bitcast_add_fusion.8
  843.7 1.3 reduce
  845.2 12.6 %all_to_all.18 = f32[8,1,4096]{2,1,0:T(1,128)S(1)} all-to-all(f32[8,1,4096]{2,1,0:T(1,128)S(1)} %reshape.99), channel_id=1, replica_groups=mesh['gz'=96,'ta'=8] {'ta'}, dimensions={0} | all-to-all | bytes 262144 | tf_op jit(solution)/shard_map/all_to_all | solution.py:114
  (139 shorter events, 102.2 us)
Async XLA Ops:
  6.5 836.4 %copy-start.1 = (f32[1,64,512]{2,1,0:T(8,128)S(1)}, f32[1,64,512]{2,1,0:T(8,128)}, u32[]{:S(2)}) copy-start(f32[1,64,512]{2,1,0:T(8,128)} %param.9) | copy-start | bytes 393220
  6.5 163.1 %all-gather.10.cloned.1.call-start = ((), (), s32[]{:S(2)}) async-start(), calls=%async_computation.2 | async-start | bytes 12713984 | tf_op jit(solution)/shard_map/all_gather | solution.py:27
  10.0 466.3 %copy-start = (f32[64,512]{1,0:T(8,128)S(1)}, f32[64,512]{1,0:T(8,128)}, u32[]{:S(2)}) copy-start(f32[64,512]{1,0:T(8,128)} %get-tuple-element.210) | copy-start | bytes 393220
  10.0 312.9 %all-gather.12.cloned.1.call-start = ((), (), s32[]{:S(2)}) async-start(), calls=%async_computation.3 | async-start | bytes 12713984 | tf_op jit(solution)/shard_map/all_gather | solution.py:27
  10.7 465.5 %all-gather.8.cloned.1.call-start = ((), (), s32[]{:S(2)}) async-start(), calls=%async_computation.1 | async-start | bytes 12713984 | tf_op jit(solution)/shard_map/all_gather | solution.py:27
  12.1 19.3 %collective-permute-start.2 = (f32[1,8,512]{2,1,0:T(8,128)S(1)}, f32[1,8,512]{2,1,0:T(8,128)S(1)}, u32[]{:S(2)}, u32[]{:S(2)}) collective-permute-start(f32[1,8,512]{2,1,0:T(8,128)S(1)} %get-tuple-element.229), channel_id=1, source_target_pairs={{0,1},{1,2},{2,3},{3,4},{4,5},{5,6},{6,7},{8,9},{9,10},{10,11},{11... | collective-permute-start | bytes 49160 | tf_op jit(solution)/shard_map/ppermute | solution.py:17
  16.7 14.8 %collective-permute-start.3 = (f32[1,8,512]{2,1,0:T(8,128)S(1)}, f32[1,8,512]{2,1,0:T(8,128)S(1)}, u32[]{:S(2)}, u32[]{:S(2)}) collective-permute-start(f32[1,8,512]{2,1,0:T(8,128)S(1)} %get-tuple-element.230), channel_id=1, source_target_pairs={{1,0},{2,1},{3,2},{4,3},{5,4},{6,5},{7,6},{9,8},{10,9},{11,10},{12... | collective-permute-start | bytes 49160 | tf_op jit(solution)/shard_map/ppermute | solution.py:18
  27.1 4.6 collective-permute-start
  29.0 5.1 collective-permute-start.1
  34.7 4.3 collective-permute-start.4
  36.6 5.5 collective-permute-start.5
  42.7 4.3 collective-permute-start.6
  44.6 5.5 collective-permute-start.7
  50.7 4.3 collective-permute-start.8
  52.6 5.4 collective-permute-start.9
  58.6 4.3 collective-permute-start.10
  60.5 5.5 collective-permute-start.11
  66.6 4.3 collective-permute-start.12
  68.5 5.5 collective-permute-start.13
  74.6 4.3 collective-permute-start.14
  76.5 5.1 collective-permute-start.15
  83.4 648.7 %all-gather.14.cloned.1.call-start = ((), (), s32[]{:S(2)}) async-start(), calls=%async_computation.4 | async-start | bytes 12713984 | tf_op jit(solution)/shard_map/all_gather | solution.py:27
Sparse Core Ops, SparseCore 0:
  11.1 158.4 all-gather.9
  173.4 149.5 all-gather.11
  326.7 149.4 all-gather.7
  479.8 252.1 all-gather.13
where the time goes:
time: 869 us; the launch traced here: 867 us
  waiting for transfers between devices  669 us (77%)
  other arithmetic  115 us (13%)
  starting transfers between devices  44.1 us (5%)
  between operations  13.6 us (2%)
  blocking collectives  12.6 us (1%)
    all_gather x4, waiting for transfers between devices, carried_in(): gathered = jax.tree.map(lambda a: lax.all_gather(a, axis), part)  648 us
    add x95, other arithmetic, affine_join(): latter[0] * earlier[2] + latter[2]  108 us
    ppermute x8, starting transfers between devices, padded(): after = lax.ppermute(initial, axis, down)  26 us
    ppermute x8, waiting for transfers between devices, padded(): after = lax.ppermute(initial, axis, down)  20.2 us
    ppermute x8, starting transfers between devices, padded(): before = lax.ppermute(last, axis, up)  18 us
  transfers between devices with their start and end apart: 20, of which 11 were waited for; matrix products, arithmetic and copies ran while one was open for 1% of the time, Pallas kernels for 0%

commit v1 on v0

v1 whole, which is shorter than its diff:
```python
import jax
import jax.numpy as jnp
from jax import lax
from jax.experimental import pallas as pl
from jax.experimental.pallas import tpu as pltpu
from jax.sharding import PartitionSpec as P

RADIUS = 8
PASSES = 7
HALO = RADIUS * PASSES
LANES = 128
F32 = jnp.float32
BF16 = jnp.bfloat16
VM = pl.BlockSpec(memory_space=pltpu.VMEM)
SM = pl.BlockSpec(memory_space=pltpu.SMEM)


def edges_body(log_ref, mask_ref, cov_ref, first_ref, last_ref):
    rows = log_ref.shape[0]
    weight = 1.0 + mask_ref[...].astype(F32) * cov_ref[...].astype(F32)
    first_ref[0] = weight[:HALO]
    first_ref[1] = log_ref[:HALO]
    last_ref[0] = weight[rows - HALO:]
    last_ref[1] = log_ref[rows - HALO:]


def halves(values):
    high = values.astype(BF16)
    return high, (values - high.astype(F32)).astype(BF16)


def box(values, col_band, row_band):
    high, low = halves(values)
    cols = jnp.dot(high, col_band, preferred_element_type=F32) + jnp.dot(
        low, col_band, preferred_element_type=F32
    )
    rows_in = values.shape[0]
    rows_out = rows_in - 2 * RADIUS
    band = row_band[:rows_out, :rows_in]
    high, low = halves(cols)
    return jnp.dot(band, high, preferred_element_type=F32) + jnp.dot(
        band, low, preferred_element_type=F32
    )


def to_tiles(out_ref, values):
    rows, cols = values.shape
    place = 0
    for r in range(0, rows, 8):
        for c in range(0, cols, LANES):
            out_ref[place:place + 8, :] = values[r:r + 8, c:c + LANES]
            place += 8
    if place < out_ref.shape[0]:
        out_ref[place:, :] = jnp.zeros((out_ref.shape[0] - place, LANES), F32)


def smooth_body(log_ref, mask_ref, cov_ref, above_ref, below_ref, cb_ref, rb_ref, s_ref, e_ref):
    rows = log_ref.shape[0]
    own = 1.0 + mask_ref[...].astype(F32) * cov_ref[...].astype(F32)
    weight = jnp.concatenate([above_ref[0], own, below_ref[0]], axis=0)
    field = jnp.concatenate([above_ref[1], log_ref[...], below_ref[1]], axis=0)
    col_band = cb_ref[...]
    row_band = rb_ref[...]
    denom = jnp.maximum(box(weight, col_band, row_band), 1.0)
    inverse = 1.0 / denom
    total = rows + 2 * HALO
    scale = weight[RADIUS:total - RADIUS] * inverse
    now = weight * field
    trim = 0
    for level in range(PASSES):
        now = box(now, col_band, row_band)
        if level < PASSES - 1:
            now = now * scale[trim:scale.shape[0] - trim]
            trim += RADIUS
    smoothed = now * inverse[trim:inverse.shape[0] - trim]
    to_tiles(s_ref, smoothed)
    to_tiles(e_ref, log_ref[...] - smoothed)


def norms_body(keep_ref, fade_ref, fore_ref, back_ref):
    sections = keep_ref.shape[0]
    wide = fade_ref.shape[0]
    fade = fade_ref[...]
    norm = jnp.zeros_like(fade)
    for z in range(sections):
        decay = keep_ref[z] * fade
        gain = 1.0 - decay
        norm = decay * norm + gain
        fore_ref[z * wide:(z + 1) * wide, :] = gain / norm
    norm = jnp.zeros_like(fade)
    for z in reversed(range(sections)):
        decay = keep_ref[z] * fade
        norm = decay * norm + (1.0 - decay)
        back_ref[z * wide:(z + 1) * wide, :] = 1.0 / norm


def scan_body(keep_ref, fade_ref, fore_ref, back_ref, s_ref, out_ref):
    sections = keep_ref.shape[0]
    wide = fade_ref.shape[0]
    fade = fade_ref[...]
    mass = jnp.zeros_like(fade)
    for z in range(sections):
        decay = keep_ref[z] * fade
        at = slice(z * wide, (z + 1) * wide)
        mass = decay * mass + (1.0 - decay) * s_ref[at, :]
        out_ref[at, :] = mass * fore_ref[at, :]
    mass = jnp.zeros_like(fade)
    for z in reversed(range(sections)):
        decay = keep_ref[z] * fade
        at = slice(z * wide, (z + 1) * wide)
        mass = decay * mass + out_ref[at, :]
        out_ref[at, :] = mass * back_ref[at, :]


def pack_body(e_ref, drift_ref, out_ref):
    half = LANES // 2
    tiles = e_ref.shape[0] // 8
    across = out_ref.shape[0] * LANES // (tiles * 8 * LANES)
    del across
    blocks = out_ref.shape[0]
    per_row = blocks // 2
    row_tiles = tiles // per_row
    for c in range(per_row):
        for r in range(row_tiles // 2):
            top = (r * per_row + c) * 8
            low = ((r + row_tiles // 2) * per_row + c) * 8
            a = e_ref[top:top + 8, :] + drift_ref[top:top + 8, :]
            b = e_ref[low:low + 8, :] + drift_ref[low:low + 8, :]
            lane = lax.broadcasted_iota(jnp.int32, a.shape, 1) < half
            out_ref[2 * c, r * 8:(r + 1) * 8, :] = jnp.where(lane, a, pltpu.roll(b, half, 1))
            out_ref[2 * c + 1, r * 8:(r + 1) * 8, :] = jnp.where(lane, pltpu.roll(a, half, 1), b)


def unpack_body(in_ref, out_ref):
    half = LANES // 2
    blocks, depth, _ = in_ref.shape
    for t in range(blocks):
        values = in_ref[t]
        start = 2 * depth * t
        out_ref[start:start + depth, :] = values[:, :half]
        out_ref[start + depth:start + 2 * depth, :] = values[:, half:]


def shards(log_mean, tile_mask, coverage, lifetime, keep):
    rows, cols = log_mean.shape[1:]
    sections = keep.shape[0]
    size = lax.axis_size("ta")
    log2, mask2, cov2 = log_mean[0], tile_mask[0], coverage[0]
    edge = jax.ShapeDtypeStruct((2, HALO, cols), F32)
    first, last = pl.pallas_call(
        edges_body, out_shape=(edge, edge), in_specs=[VM] * 3, out_specs=(VM, VM), name="edges"
    )(log2, mask2, cov2)
    up = [(i, i + 1) for i in range(size - 1)]
    down = [(j, i) for i, j in up]
    above = lax.ppermute(last, "ta", up)
    below = lax.ppermute(first, "ta", down)

    used = rows * cols // LANES
    wide = -(-used // sections)
    padded = sections * wide
    tiled = lifetime.reshape(rows // 8, 8, cols // LANES, LANES).transpose(0, 2, 1, 3)
    tiled = jnp.pad(tiled.reshape(used, LANES), ((0, padded - used), (0, 0)), constant_values=1.0)
    mine = lax.dynamic_slice_in_dim(tiled, lax.axis_index("gz") * wide, wide)
    fade = jnp.exp(-mine / sections)
    long = jax.ShapeDtypeStruct((padded, LANES), F32)
    fore, back = pl.pallas_call(
        norms_body, out_shape=(long, long), in_specs=[SM, VM], out_specs=(VM, VM), name="norms"
    )(keep, fade)

    place = jnp.arange(cols)
    col_band = (jnp.abs(place[:, None] - place[None, :]) <= RADIUS).astype(BF16)
    total = rows + 2 * HALO
    offset = jnp.arange(total)[None, :] - jnp.arange(total - 2 * RADIUS)[:, None]
    row_band = ((offset >= 0) & (offset <= 2 * RADIUS)).astype(BF16)
    smoothed, rest = pl.pallas_call(
        smooth_body,
        out_shape=(long, jax.ShapeDtypeStruct((used, LANES), F32)),
        in_specs=[VM] * 7,
        out_specs=(VM, VM),
        name="smooth",
    )(log2, mask2, cov2, above, below, col_band, row_band)

    def swap(values):
        flat = values.reshape(padded * LANES)
        flat = lax.all_to_all(flat, "gz", 0, 0, tiled=True)
        return flat.reshape(padded, LANES)

    drift = pl.pallas_call(
        scan_body, out_shape=long, in_specs=[SM] + [VM] * 4, out_specs=VM, name="scan"
    )(keep, fade, fore, back, swap(smoothed))
    drift = swap(drift)
    packed = pl.pallas_call(
        pack_body,
        out_shape=jax.ShapeDtypeStruct((size, used // size, LANES), F32),
        in_specs=[VM] * 2,
        out_specs=VM,
        name="pack",
    )(rest, drift)
    packed = lax.all_to_all(packed, "ta", 0, 0, tiled=True)
    out = pl.pallas_call(
        unpack_body,
        out_shape=jax.ShapeDtypeStruct((size * rows, cols // size), F32),
        in_specs=[VM],
        out_specs=VM,
        name="unpack",
    )(packed)
    return out[None]


def solution(mesh):
    return jax.shard_map(
        shards,
        mesh=mesh,
        in_specs=(
            P("gz", "ta", None),
            P("gz", "ta", None),
            P("gz", "ta", None),
            P("ta", None),
            P(),
        ),
        out_specs=P("gz", None, "ta"),
        check_vma=False,
    )
```

time: 869 us -> 99.4 us (0.11)
  waiting for transfers between devices: 669 us -> 11.6 us
  other arithmetic: 115 us -> 2.13 us
  blocking collectives: 12.6 us -> 34.8 us
  Pallas kernels: 0 us -> 14.9 us
  between operations: 13.6 us -> 0.06 us
  starting transfers between devices: 44.1 us -> 31.7 us
    all_gather x4 -> x0, waiting for transfers between devices: 648 us -> none  [carried_in(): gathered = jax.tree.map(lambda a: lax.all_gather(a, axis), part)]
    add x99 -> x0, other arithmetic: 112 us -> none  [the longest x95 108 us: affine_join(): latter[0] * earlier[2] + latter[2]]
    ppermute x16 -> x2, starting transfers between devices: 43.9 us -> 13.7 us  [the longest x1 9.19 us: shards(): below = lax.ppermute(first, 'ta', down)]
    all_to_all x1 -> x2, blocking collectives: 12.6 us -> 34.8 us  [the longest x1 20.9 us: swap(): flat = lax.all_to_all(flat, 'gz', 0, 0, tiled=True)]
    ppermute x16 -> x2, waiting for transfers between devices: 20.2 us -> 0.01 us  [the longest x1 0.01 us: shards(): above = lax.ppermute(last, 'ta', up)]
    all_to_all x0 -> x1, starting transfers between devices: none -> 18 us  [swap(): flat = lax.all_to_all(flat, 'gz', 0, 0, tiled=True)]
    pallas_call x0 -> x6, Pallas kernels: none -> 14.9 us  [the longest x1 5.82 us: shards(): pl.pallas_call(smooth_body, out_shape=(long, jax.ShapeDtypeStruct((used,...]
    all_to_all x0 -> x1, waiting for transfers between devices: none -> 11.6 us  [swap(): flat = lax.all_to_all(flat, 'gz', 0, 0, tiled=True)]
  transfers between devices with their start and end apart: 20 -> 3, of which waited for: 11 -> 1; matrix products, arithmetic and copies ran while one was open for 1% -> 2% of each run, Pallas kernels for 0% -> 2%
where the time goes in v1:
time: 99.4 us; the launch traced here: 98.9 us
  blocking collectives  34.8 us (35%)
  starting transfers between devices  31.7 us (32%)
  Pallas kernels  14.9 us (15%)
  waiting for transfers between devices  11.6 us (12%)
  local copies, waits for them, and re-layouts  3.75 us (4%)
  other arithmetic  2.13 us (2%)
    all_to_all x1, blocking collectives, swap(): flat = lax.all_to_all(flat, 'gz', 0, 0, tiled=True)  20.9 us
    all_to_all x1, starting transfers between devices, swap(): flat = lax.all_to_all(flat, 'gz', 0, 0, tiled=True)  18 us
    all_to_all x1, blocking collectives, shards(): packed = lax.all_to_all(packed, 'ta', 0, 0, tiled=True)  13.9 us
    all_to_all x1, waiting for transfers between devices, swap(): flat = lax.all_to_all(flat, 'gz', 0, 0, tiled=True)  11.6 us
    ppermute x1, starting transfers between devices, shards(): below = lax.ppermute(first, 'ta', down)  9.19 us
    pallas_call x1, Pallas kernels, shards(): pl.pallas_call(smooth_body, out_shape=(long, jax.ShapeDtypeStruct((used,...  5.82 us
    ppermute x1, starting transfers between devices, shards(): above = lax.ppermute(last, 'ta', up)  4.49 us
    pallas_call x1, Pallas kernels, shards(): pl.pallas_call(scan_body, out_shape=long, in_specs=[SM] + [VM] * 4, out_s...  2.15 us
  transfers between devices with their start and end apart: 3, of which 1 were waited for; matrix products, arithmetic and copies ran while one was open for 2% of the time, Pallas kernels for 2%

profile of v1, /device:TPU:1, one launch (start us, length us, event | category | flops | bytes accessed | tf_op | source)
XLA Modules:
  0.0 98.9 jit_solution(69616083227360638)
XLA Ops:
  0.0 1.8 %edges.1 = (f32[2,56,512]{2,1,0:T(8,128)}, f32[2,56,512]{2,1,0:T(8,128)}) custom-call(f32[64,512]{1,0:T(8,128)} %bitcast.17, s32[64,512]{1,0:T(8,128)} %bitcast.19, s32[64,512]{1,0:T(8,128)} %bitcast.21), custom_call_target="tpu_custom_call" | custom-call | tf_op jit(solution)/shard_map/edges/pallas_call | solution.py:150
  1.8 4.5 %collective-permute-start = (f32[2,56,512]{2,1,0:T(8,128)}, f32[2,56,512]{2,1,0:T(8,128)S(1)}, u32[]{:S(2)}, u32[]{:S(2)}) collective-permute-start(f32[2,56,512]{2,1,0:T(8,128)} %get-tuple-element.11), channel_id=1, source_target_pairs={{0,1},{1,2},{2,3},{3,4},{4,5},{5,6},{6,7},{8,9},{9,10},{10,11},{11... | collective-permute-start | bytes 688136 | tf_op jit(solution)/shard_map/ppermute | solution.py:155
  6.3 9.2 %collective-permute-start.1 = (f32[2,56,512]{2,1,0:T(8,128)}, f32[2,56,512]{2,1,0:T(8,128)S(1)}, u32[]{:S(2)}, u32[]{:S(2)}) collective-permute-start(f32[2,56,512]{2,1,0:T(8,128)} %get-tuple-element.12), channel_id=1, source_target_pairs={{1,0},{2,1},{3,2},{4,3},{5,4},{6,5},{7,6},{9,8},{10,9},{11,10},{12... | collective-permute-start | bytes 688136 | tf_op jit(solution)/shard_map/ppermute | solution.py:156
  15.5 0.7 fusion.4.rb_ref
  16.2 0.9 fusion.cb_ref
  17.1 0.0 collective-permute-done.above_ref
  17.1 0.0 copy-start.1
  17.1 0.0 collective-permute-done.1.below_ref
  17.1 0.7 copy-done.1
  17.8 0.0 copy-start.2
  17.8 0.7 copy-done.2
  18.4 5.8 %smooth.1 = (f32[288,128]{1,0:T(8,128)}, f32[256,128]{1,0:T(8,128)}) custom-call(f32[64,512]{1,0:T(8,128)} %bitcast.18, s32[64,512]{1,0:T(8,128)} %bitcast.20, s32[64,512]{1,0:T(8,128)} %bitcast.22, f32[2,56,512]{2,1,0:T(8,128)} %copy-done.1, f32[2,56,512]{2,1,0:T(8,128)} %copy-done.2, bf16[512,512]{1,0:T(8,128)(2,1)} %fusion.cb_ref, ...), custom_call_target="tpu_custom_call" | custom-call | tf_op jit(solution)/shard_map/smooth/pallas_call | solution.py:175
  24.3 0.0 copy-start.3
  24.3 18.0 %all-to-all-start = ((f32[96,384,1]{1,2,0:T(1,128)}), f32[96,384,1]{1,2,0:T(1,128)S(1)}, u32[]{:S(2)}, u32[]{:S(2)}) async-start(f32[96,384,1]{1,2,0:T(1,128)} %bitcast.23), calls=%async_computation | async-start | bytes 294912 | tf_op jit(solution)/shard_map/all_to_all | solution.py:185
  42.3 0.0 copy-done.3
  42.3 0.6 multiply_exponential_fusion.fade_ref
  42.9 1.6 %norms.1 = (f32[288,128]{1,0:T(8,128)}, f32[288,128]{1,0:T(8,128)}) custom-call(f32[96]{0:T(128)} %keep_ref.3, f32[3,128]{1,0:T(4,128)} %multiply_exponential_fusion.fade_ref), custom_call_target="tpu_custom_call" | custom-call | tf_op jit(solution)/shard_map/norms/pallas_call | solution.py:166
  44.5 11.6 %all-to-all-done = f32[96,384,1]{1,2,0:T(1,128)S(1)} async-done(((f32[96,384,1]{1,2,0:T(1,128)}), f32[96,384,1]{1,2,0:T(1,128)S(1)}, u32[]{:S(2)}, u32[]{:S(2)}) %all-to-all-start) | async-done | bytes 147488 | tf_op jit(solution)/shard_map/all_to_all | solution.py:185
  56.1 0.0 copy-start
  56.1 0.7 copy-done
  56.7 2.2 %scan.1 = f32[288,128]{1,0:T(8,128)} custom-call(f32[96]{0:T(128)} %keep_ref.3, f32[3,128]{1,0:T(4,128)} %multiply_exponential_fusion.fade_ref, f32[288,128]{1,0:T(8,128)} %get-tuple-element.14.fore_ref, f32[288,128]{1,0:T(8,128)} %get-tuple-element.15.back_ref, f32[288,128]{1,0:T(8,128)} %bitcast.15), custom_call_target="tpu_custom_call" | custom-call | tf_op jit(solution)/shard_map/scan/pallas_call | solution.py:188
  58.9 20.9 %all_to_all.23 = f32[96,384,1]{1,2,0:T(1,128)} all-to-all(f32[96,384,1]{1,2,0:T(1,128)} %bitcast.16), channel_id=1, replica_groups=mesh['gz'=96,'ta'=8] {'gz'}, dimensions={0} | all-to-all | bytes 294912 | tf_op jit(solution)/shard_map/all_to_all | solution.py:185
  79.8 1.7 %pack.1 = f32[8,32,128]{2,1,0:T(8,128)} custom-call(f32[256,128]{1,0:T(8,128)} %get-tuple-element.13.e_ref, f32[288,128]{1,0:T(8,128)} %bitcast.14), custom_call_target="tpu_custom_call" | custom-call | tf_op jit(solution)/shard_map/pack/pallas_call | solution.py:192
  81.5 13.9 %all_to_all.24.in_ref = f32[8,32,128]{2,1,0:T(8,128)} all-to-all(f32[8,32,128]{2,1,0:T(8,128)} %pack.1), channel_id=1, replica_groups=mesh['gz'=96,'ta'=8] {'ta'}, dimensions={0} | all-to-all | bytes 262144 | tf_op jit(solution)/shard_map/all_to_all | solution.py:199
  95.4 1.7 %unpack.1 = f32[512,64]{1,0:T(8,128)} custom-call(f32[8,32,128]{2,1,0:T(8,128)} %all_to_all.24.in_ref), custom_call_target="tpu_custom_call" | custom-call | tf_op jit(solution)/shard_map/unpack/pallas_call | solution.py:200
  97.1 1.7 %copy.9 = f32[1,512,64]{1,2,0:T(8,128)} copy(f32[1,512,64]{2,1,0:T(8,128)} %bitcast.13) | data formatting | bytes 262144 | tf_op jit(solution)/shard_map/broadcast_in_dim | solution.py:207
Async XLA Ops:
  1.8 15.2 %collective-permute-start = (f32[2,56,512]{2,1,0:T(8,128)}, f32[2,56,512]{2,1,0:T(8,128)S(1)}, u32[]{:S(2)}, u32[]{:S(2)}) collective-permute-start(f32[2,56,512]{2,1,0:T(8,128)} %get-tuple-element.11), channel_id=1, source_target_pairs={{0,1},{1,2},{2,3},{3,4},{4,5},{5,6},{6,7},{8,9},{9,10},{10,11},{11... | collective-permute-start | bytes 688136 | tf_op jit(solution)/shard_map/ppermute | solution.py:155
  6.3 10.7 %collective-permute-start.1 = (f32[2,56,512]{2,1,0:T(8,128)}, f32[2,56,512]{2,1,0:T(8,128)S(1)}, u32[]{:S(2)}, u32[]{:S(2)}) collective-permute-start(f32[2,56,512]{2,1,0:T(8,128)} %get-tuple-element.12), channel_id=1, source_target_pairs={{1,0},{2,1},{3,2},{4,3},{5,4},{6,5},{7,6},{9,8},{10,9},{11,10},{12... | collective-permute-start | bytes 688136 | tf_op jit(solution)/shard_map/ppermute | solution.py:156
  17.1 0.7 copy-start.1
  17.8 0.7 copy-start.2
  24.3 18.0 %copy-start.3 = (f32[64,512]{1,0:T(8,128)S(1)}, f32[64,512]{1,0:T(8,128)}, u32[]{:S(2)}) copy-start(f32[64,512]{1,0:T(8,128)} %param.8) | copy-start | bytes 393220
  24.3 31.8 %all-to-all-start = ((f32[96,384,1]{1,2,0:T(1,128)}), f32[96,384,1]{1,2,0:T(1,128)S(1)}, u32[]{:S(2)}, u32[]{:S(2)}) async-start(f32[96,384,1]{1,2,0:T(1,128)} %bitcast.23), calls=%async_computation | async-start | bytes 294912 | tf_op jit(solution)/shard_map/all_to_all | solution.py:185
  56.1 0.7 copy-start

commit v2 on v1

--- a/solution.py
+++ b/solution.py
@@ -148,7 +148,7 @@
     log2, mask2, cov2 = log_mean[0], tile_mask[0], coverage[0]
     edge = jax.ShapeDtypeStruct((2, HALO, cols), F32)
     first, last = pl.pallas_call(
-        edges_body, out_shape=(edge, edge), in_specs=[VM] * 3, out_specs=(VM, VM), name="edges"
+        edges_body, out_shape=(edge, edge), in_specs=[VM] * 3, out_specs=(VM, VM), name="edges", compiler_params=pltpu.CompilerParams(vmem_limit_bytes=16<<20)
     )(log2, mask2, cov2)
     up = [(i, i + 1) for i in range(size - 1)]
     down = [(j, i) for i, j in up]
@@ -164,7 +164,7 @@
     fade = jnp.exp(-mine / sections)
     long = jax.ShapeDtypeStruct((padded, LANES), F32)
     fore, back = pl.pallas_call(
-        norms_body, out_shape=(long, long), in_specs=[SM, VM], out_specs=(VM, VM), name="norms"
+        norms_body, out_shape=(long, long), in_specs=[SM, VM], out_specs=(VM, VM), name="norms", compiler_params=pltpu.CompilerParams(vmem_limit_bytes=16<<20)
     )(keep, fade)
 
     place = jnp.arange(cols)
@@ -177,7 +177,7 @@
         out_shape=(long, jax.ShapeDtypeStruct((used, LANES), F32)),
         in_specs=[VM] * 7,
         out_specs=(VM, VM),
-        name="smooth",
+        name="smooth", compiler_params=pltpu.CompilerParams(vmem_limit_bytes=16<<20),
     )(log2, mask2, cov2, above, below, col_band, row_band)
 
     def swap(values):
@@ -186,7 +186,7 @@
         return flat.reshape(padded, LANES)
 
     drift = pl.pallas_call(
-        scan_body, out_shape=long, in_specs=[SM] + [VM] * 4, out_specs=VM, name="scan"
+        scan_body, out_shape=long, in_specs=[SM] + [VM] * 4, out_specs=VM, name="scan", compiler_params=pltpu.CompilerParams(vmem_limit_bytes=16<<20)
     )(keep, fade, fore, back, swap(smoothed))
     drift = swap(drift)
     packed = pl.pallas_call(
@@ -194,7 +194,7 @@
         out_shape=jax.ShapeDtypeStruct((size, used // size, LANES), F32),
         in_specs=[VM] * 2,
         out_specs=VM,
-        name="pack",
+        name="pack", compiler_params=pltpu.CompilerParams(vmem_limit_bytes=16<<20),
     )(rest, drift)
     packed = lax.all_to_all(packed, "ta", 0, 0, tiled=True)
     out = pl.pallas_call(
@@ -202,7 +202,7 @@
         out_shape=jax.ShapeDtypeStruct((size * rows, cols // size), F32),
         in_specs=[VM],
         out_specs=VM,
-        name="unpack",
+        name="unpack", compiler_params=pltpu.CompilerParams(vmem_limit_bytes=16<<20),
     )(packed)
     return out[None]
 

time: 99.4 us -> 90 us (0.905)
  Pallas kernels: 14.9 us -> 6.36 us
  other arithmetic: 2.13 us -> 0.12 us
  waiting for transfers between devices: 11.6 us -> 13.4 us
  blocking collectives: 34.8 us -> 33 us
    pallas_call x1, Pallas kernels: 1.84 us -> 0.03 us  [shards(): pl.pallas_call(edges_body, out_shape=(edge, edge), in_specs=[VM] * 3, out...]
    pallas_call x1, Pallas kernels: 1.73 us -> 0.1 us  [shards(): pl.pallas_call(pack_body, out_shape=jax.ShapeDtypeStruct((size, used // s...]
    pallas_call x1, Pallas kernels: 1.71 us -> 0.09 us  [shards(): pl.pallas_call(unpack_body, out_shape=jax.ShapeDtypeStruct((size * rows,...]
    all_to_all x1, blocking collectives: 20.9 us -> 19.4 us  [swap(): flat = lax.all_to_all(flat, 'gz', 0, 0, tiled=True)]
    pallas_call x1, Pallas kernels: 5.82 us -> 4.38 us  [shards(): pl.pallas_call(smooth_body, out_shape=(long, jax.ShapeDtypeStruct((used,...]
    unnamed x8 -> x10, local copies, waits for them, and re-layouts: 2.03 us -> 3.34 us
    pallas_call x1, Pallas kernels: 2.15 us -> 0.96 us  [shards(): pl.pallas_call(scan_body, out_shape=long, in_specs=[SM] + [VM] * 4, out_s...]
  transfers between devices with their start and end apart: 3 -> 3, of which waited for: 1 -> 2; matrix products, arithmetic and copies ran while one was open for 2% -> 0% of each run, Pallas kernels for 2% -> 1%
where the time goes in v2:
time: 90 us; the launch traced here: 89.6 us
  blocking collectives  33 us (37%)
  starting transfers between devices  32.6 us (36%)
  waiting for transfers between devices  13.4 us (15%)
  Pallas kernels  6.36 us (7%)
  local copies, waits for them, and re-layouts  4.12 us (5%)
    all_to_all x1, blocking collectives, swap(): flat = lax.all_to_all(flat, 'gz', 0, 0, tiled=True)  19.4 us
    all_to_all x1, starting transfers between devices, swap(): flat = lax.all_to_all(flat, 'gz', 0, 0, tiled=True)  18.9 us
    all_to_all x1, blocking collectives, shards(): packed = lax.all_to_all(packed, 'ta', 0, 0, tiled=True)  13.5 us
    all_to_all x1, waiting for transfers between devices, swap(): flat = lax.all_to_all(flat, 'gz', 0, 0, tiled=True)  12.4 us
    ppermute x1, starting transfers between devices, shards(): below = lax.ppermute(first, 'ta', down)  9.19 us
    ppermute x1, starting transfers between devices, shards(): above = lax.ppermute(last, 'ta', up)  4.5 us
    pallas_call x1, Pallas kernels, shards(): pl.pallas_call(smooth_body, out_shape=(long, jax.ShapeDtypeStruct((used,...  4.38 us
    unnamed x10, local copies, waits for them, and re-layouts  3.34 us
  transfers between devices with their start and end apart: 3, of which 2 were waited for; matrix products, arithmetic and copies ran while one was open for 0% of the time, Pallas kernels for 1%

profile of v2, /device:TPU:1, one launch (start us, length us, event | category | flops | bytes accessed | tf_op | source)
XLA Modules:
  0.0 89.6 jit_solution(15171703194813011794)
XLA Ops:
  0.0 0.0 copy-start
  0.0 0.9 %copy-done = f32[1,64,512]{2,1,0:T(8,128)S(1)} copy-done((f32[1,64,512]{2,1,0:T(8,128)S(1)}, f32[1,64,512]{2,1,0:T(8,128)}, u32[]{:S(2)}) %copy-start) | copy-done | bytes 131096
  0.9 0.0 copy-start.1
  0.9 0.9 %copy-done.1 = s32[1,64,512]{2,1,0:T(8,128)S(1)} copy-done((s32[1,64,512]{2,1,0:T(8,128)S(1)}, s32[1,64,512]{2,1,0:T(8,128)}, u32[]{:S(2)}) %copy-start.1) | copy-done | bytes 131096
  1.8 0.0 copy-start.2
  1.8 0.9 %copy-done.2 = s32[1,64,512]{2,1,0:T(8,128)S(1)} copy-done((s32[1,64,512]{2,1,0:T(8,128)S(1)}, s32[1,64,512]{2,1,0:T(8,128)}, u32[]{:S(2)}) %copy-start.2) | copy-done | bytes 131096
  2.8 4.5 %collective-permute-start = (f32[2,56,512]{2,1,0:T(8,128)S(1)}, f32[2,56,512]{2,1,0:T(8,128)S(1)}, u32[]{:S(2)}, u32[]{:S(2)}) collective-permute-start(f32[2,56,512]{2,1,0:T(8,128)S(1)} %get-tuple-element.11), channel_id=1, source_target_pairs={{0,1},{1,2},{2,3},{3,4},{4,5},{5,6},{6,7},{8,9},{9,10},{10,11},{11... | collective-permute-start | bytes 688136 | tf_op jit(solution)/shard_map/ppermute | solution.py:155
  7.3 9.2 %collective-permute-start.1 = (f32[2,56,512]{2,1,0:T(8,128)S(1)}, f32[2,56,512]{2,1,0:T(8,128)S(1)}, u32[]{:S(2)}, u32[]{:S(2)}) collective-permute-start(f32[2,56,512]{2,1,0:T(8,128)S(1)} %get-tuple-element.12), channel_id=1, source_target_pairs={{1,0},{2,1},{3,2},{4,3},{5,4},{6,5},{7,6},{9,8},{10,9},{11,10},{12... | collective-permute-start | bytes 688136 | tf_op jit(solution)/shard_map/ppermute | solution.py:156
  16.5 0.1 fusion.cb_ref
  16.6 0.0 collective-permute-done.above_ref
  16.6 1.0 %collective-permute-done.1.below_ref = f32[2,56,512]{2,1,0:T(8,128)S(1)} collective-permute-done((f32[2,56,512]{2,1,0:T(8,128)S(1)}, f32[2,56,512]{2,1,0:T(8,128)S(1)}, u32[]{:S(2)}, u32[]{:S(2)}) %collective-permute-start.1) | collective-permute-done | bytes 229408 | tf_op jit(solution)/shard_map/ppermute | solution.py:156
  17.6 4.4 %smooth.1 = (f32[288,128]{1,0:T(8,128)}, f32[256,128]{1,0:T(8,128)S(1)}) custom-call(f32[64,512]{1,0:T(8,128)S(1)} %bitcast.18, s32[64,512]{1,0:T(8,128)S(1)} %bitcast.20, s32[64,512]{1,0:T(8,128)S(1)} %bitcast.22, f32[2,56,512]{2,1,0:T(8,128)S(1)} %collective-permute-done.above_ref, f32[2,56,512]{2,1,0:T(8,128)S(1)} %collective-permute-done.1.below_ref, ...), custom_call_target="tpu_custom_call" | custom-call | tf_op jit(solution)/shard_map/smooth/pallas_call | solution.py:175
  21.9 0.0 copy-start.4
  21.9 18.9 %all-to-all-start = ((f32[96,384,1]{1,2,0:T(1,128)}), f32[96,384,1]{1,2,0:T(1,128)S(1)}, u32[]{:S(2)}, u32[]{:S(2)}) async-start(f32[96,384,1]{1,2,0:T(1,128)} %bitcast.6), calls=%async_computation | async-start | bytes 294912 | tf_op jit(solution)/shard_map/all_to_all | solution.py:185
  40.9 0.0 copy-done.4
  40.9 0.0 copy-start.3
  40.9 0.6 copy-done.3
  41.5 0.8 norms.1
  42.3 12.4 %all-to-all-done = f32[96,384,1]{1,2,0:T(1,128)S(1)} async-done(((f32[96,384,1]{1,2,0:T(1,128)}), f32[96,384,1]{1,2,0:T(1,128)S(1)}, u32[]{:S(2)}, u32[]{:S(2)}) %all-to-all-start) | async-done | bytes 147488 | tf_op jit(solution)/shard_map/all_to_all | solution.py:185
  54.7 1.0 %scan.1 = f32[288,128]{1,0:T(8,128)S(1)} custom-call(f32[96]{0:T(128)S(1)} %copy-done.3, f32[3,128]{1,0:T(4,128)S(1)} %multiply_exponential_fusion.fade_ref, f32[288,128]{1,0:T(8,128)S(1)} %get-tuple-element.14.fore_ref, f32[288,128]{1,0:T(8,128)S(1)} %get-tuple-element.15.back_ref, f32[288,128]{1,0:T(8,128)S(1)} %bitcast.15), custom_call_target="tpu_custom_call" | custom-call | tf_op jit(solution)/shard_map/scan/pallas_call | solution.py:188
  55.7 19.4 %all_to_all.23 = f32[96,384,1]{1,2,0:T(1,128)S(1)} all-to-all(f32[96,384,1]{1,2,0:T(1,128)S(1)} %bitcast.16), channel_id=1, replica_groups=mesh['gz'=96,'ta'=8] {'gz'}, dimensions={0} | all-to-all | bytes 294912 | tf_op jit(solution)/shard_map/all_to_all | solution.py:185
  75.1 0.1 pack.1
  75.2 13.5 %all_to_all.24.in_ref = f32[8,32,128]{2,1,0:T(8,128)S(1)} all-to-all(f32[8,32,128]{2,1,0:T(8,128)S(1)} %pack.1), channel_id=1, replica_groups=mesh['gz'=96,'ta'=8] {'ta'}, dimensions={0} | all-to-all | bytes 262144 | tf_op jit(solution)/shard_map/all_to_all | solution.py:199
  88.8 0.1 unpack.1
  88.9 0.8 copy.9
  (3 shorter events, 0.1 us)
Async XLA Ops:
  0.0 0.9 %copy-start = (f32[1,64,512]{2,1,0:T(8,128)S(1)}, f32[1,64,512]{2,1,0:T(8,128)}, u32[]{:S(2)}) copy-start(f32[1,64,512]{2,1,0:T(8,128)} %param.5) | copy-start | bytes 393220
  0.9 0.9 %copy-start.1 = (s32[1,64,512]{2,1,0:T(8,128)S(1)}, s32[1,64,512]{2,1,0:T(8,128)}, u32[]{:S(2)}) copy-start(s32[1,64,512]{2,1,0:T(8,128)} %param.6) | copy-start | bytes 393220
  1.8 0.9 %copy-start.2 = (s32[1,64,512]{2,1,0:T(8,128)S(1)}, s32[1,64,512]{2,1,0:T(8,128)}, u32[]{:S(2)}) copy-start(s32[1,64,512]{2,1,0:T(8,128)} %param.7) | copy-start | bytes 393220
  2.8 13.8 %collective-permute-start = (f32[2,56,512]{2,1,0:T(8,128)S(1)}, f32[2,56,512]{2,1,0:T(8,128)S(1)}, u32[]{:S(2)}, u32[]{:S(2)}) collective-permute-start(f32[2,56,512]{2,1,0:T(8,128)S(1)} %get-tuple-element.11), channel_id=1, source_target_pairs={{0,1},{1,2},{2,3},{3,4},{4,5},{5,6},{6,7},{8,9},{9,10},{10,11},{11... | collective-permute-start | bytes 688136 | tf_op jit(solution)/shard_map/ppermute | solution.py:155
  7.3 10.3 %collective-permute-start.1 = (f32[2,56,512]{2,1,0:T(8,128)S(1)}, f32[2,56,512]{2,1,0:T(8,128)S(1)}, u32[]{:S(2)}, u32[]{:S(2)}) collective-permute-start(f32[2,56,512]{2,1,0:T(8,128)S(1)} %get-tuple-element.12), channel_id=1, source_target_pairs={{1,0},{2,1},{3,2},{4,3},{5,4},{6,5},{7,6},{9,8},{10,9},{11,10},{12... | collective-permute-start | bytes 688136 | tf_op jit(solution)/shard_map/ppermute | solution.py:156
  21.9 18.9 %copy-start.4 = (f32[64,512]{1,0:T(8,128)S(1)}, f32[64,512]{1,0:T(8,128)}, u32[]{:S(2)}) copy-start(f32[64,512]{1,0:T(8,128)} %param.8) | copy-start | bytes 393220
  21.9 32.8 %all-to-all-start = ((f32[96,384,1]{1,2,0:T(1,128)}), f32[96,384,1]{1,2,0:T(1,128)S(1)}, u32[]{:S(2)}, u32[]{:S(2)}) async-start(f32[96,384,1]{1,2,0:T(1,128)} %bitcast.6), calls=%async_computation | async-start | bytes 294912 | tf_op jit(solution)/shard_map/all_to_all | solution.py:185
  40.9 0.7 copy-start.3

commit v3 on v2

v3 whole, which is shorter than its diff:
```python
import jax
import jax.numpy as jnp
import numpy as np
from jax import lax
from jax.experimental import pallas as pl
from jax.experimental.pallas import tpu as pltpu
from jax.sharding import PartitionSpec as P

RADIUS = 8
PASSES = 7
HALO = RADIUS * PASSES
LANES = 128
F32 = jnp.float32
BF16 = jnp.bfloat16
VM = pl.BlockSpec(memory_space=pltpu.VMEM)
SM = pl.BlockSpec(memory_space=pltpu.SMEM)
PARAMS = pltpu.CompilerParams(vmem_limit_bytes=16 << 20)


def prepare_body(wide, log_ref, mask_ref, cov_ref, life_ref, out_ref, both_ref, life_t_ref):
    rows, cols = log_ref.shape
    parts, depth, _ = out_ref.shape
    share = cols // parts
    span = share + 2 * HALO
    weight = 1.0 + mask_ref[...].astype(F32) * cov_ref[...].astype(F32)
    both = jnp.concatenate([weight, log_ref[...]], axis=0)
    life = jnp.concatenate([life_ref[...], life_ref[...]], axis=0)
    both_ref[:HALO, :] = jnp.zeros((HALO, LANES), F32)
    both_ref[HALO + cols:, :] = jnp.zeros((HALO, LANES), F32)
    for c in range(0, cols, LANES):
        both_ref[HALO + c:HALO + c + LANES, :] = both[:, c:c + LANES].T
        life_t_ref[c:c + LANES, :] = life[:, c:c + LANES].T
    first = lax.axis_index("gz") * wide
    for t in range(parts):
        out_ref[t, :span, :] = both_ref[share * t:share * t + span, :]
        out_ref[t, span:, :] = jnp.zeros((depth - span, LANES), F32)
        for i in range(wide):
            place = share * t + (first + i) % share
            out_ref[t, span + i:span + i + 1, :] = life_t_ref[pl.ds(place, 1), :]


def halves(values):
    high = values.astype(BF16)
    return high, (values - high.astype(F32)).astype(BF16)


def box(values, col_band, row_band):
    high, low = halves(values)
    cols = jnp.dot(high, col_band, preferred_element_type=F32) + jnp.dot(
        low, col_band, preferred_element_type=F32
    )
    rows_in = values.shape[0]
    rows_out = rows_in - 2 * RADIUS
    band = row_band[:rows_out, :rows_in]
    high, low = halves(cols)
    return jnp.dot(band, high, preferred_element_type=F32) + jnp.dot(
        band, low, preferred_element_type=F32
    )


def smooth_body(wide, in_ref, cb_ref, rb_ref, s_ref, e_ref, life_ref):
    parts = in_ref.shape[0]
    half = LANES // 2
    total = rb_ref.shape[1]
    share = total - 2 * HALO
    left = lax.broadcasted_iota(jnp.int32, (total, LANES), 1) < half
    weights, fields = [], []
    for t in range(0, parts, 2):
        a = in_ref[t, :total, :]
        b = in_ref[t + 1, :total, :]
        weights.append(jnp.where(left, a, pltpu.roll(b, half, 1)))
        fields.append(jnp.where(left, pltpu.roll(a, half, 1), b))
    weight = jnp.concatenate(weights, axis=1)
    field = jnp.concatenate(fields, axis=1)

    first = lax.axis_index("gz") * wide
    left = lax.broadcasted_iota(jnp.int32, (1, LANES), 1) < half
    for i in range(wide):
        pair = 2 * jnp.minimum((first + i) // share, parts // 2 - 1)
        a = in_ref[pair, total + i:total + i + 1, :]
        b = in_ref[pair + 1, total + i:total + i + 1, :]
        life_ref[i:i + 1, :] = jnp.where(left, a, b)

    col_band = cb_ref[...]
    row_band = rb_ref[...]
    denom = jnp.maximum(box(weight, col_band, row_band), 1.0)
    inverse = 1.0 / denom
    scale = weight[RADIUS:total - RADIUS] * inverse
    now = weight * field
    trim = 0
    for level in range(PASSES):
        now = box(now, col_band, row_band)
        if level < PASSES - 1:
            now = now * scale[trim:scale.shape[0] - trim]
            trim += RADIUS
    smoothed = now * inverse[trim:inverse.shape[0] - trim]
    rest = field[HALO:HALO + share] - smoothed
    for c in range(parts // 2):
        s_ref[c * share:(c + 1) * share, :] = smoothed[:, c * LANES:(c + 1) * LANES]
        e_ref[c * share:(c + 1) * share, :] = rest[:, c * LANES:(c + 1) * LANES]
    used = e_ref.shape[0]
    s_ref[used:, :] = jnp.zeros((s_ref.shape[0] - used, LANES), F32)


def norms_body(keep_ref, life_ref, fade_ref, fore_ref, back_ref):
    sections = keep_ref.shape[0]
    wide = life_ref.shape[0]
    fade = jnp.exp(-life_ref[...] / sections)
    fade_ref[...] = fade
    norm = jnp.zeros_like(fade)
    for z in range(sections):
        decay = keep_ref[z] * fade
        gain = 1.0 - decay
        norm = decay * norm + gain
        fore_ref[z * wide:(z + 1) * wide, :] = gain / norm
    norm = jnp.zeros_like(fade)
    for z in reversed(range(sections)):
        decay = keep_ref[z] * fade
        norm = decay * norm + (1.0 - decay)
        back_ref[z * wide:(z + 1) * wide, :] = 1.0 / norm


def scan_body(keep_ref, fade_ref, fore_ref, back_ref, s_ref, out_ref):
    sections = keep_ref.shape[0]
    wide = fade_ref.shape[0]
    fade = fade_ref[...]
    mass = jnp.zeros_like(fade)
    for z in range(sections):
        decay = keep_ref[z] * fade
        at = slice(z * wide, (z + 1) * wide)
        mass = decay * mass + (1.0 - decay) * s_ref[at, :]
        out_ref[at, :] = mass * fore_ref[at, :]
    mass = jnp.zeros_like(fade)
    for z in reversed(range(sections)):
        decay = keep_ref[z] * fade
        at = slice(z * wide, (z + 1) * wide)
        mass = decay * mass + out_ref[at, :]
        out_ref[at, :] = mass * back_ref[at, :]


def finish_body(e_ref, drift_ref, out_ref):
    share = out_ref.shape[0]
    for c in range(out_ref.shape[1] // LANES):
        at = slice(c * share, (c + 1) * share)
        out_ref[:, c * LANES:(c + 1) * LANES] = e_ref[at, :] + drift_ref[at, :]


def call(body, name, outs, ins, scratch=()):
    return pl.pallas_call(
        body,
        out_shape=outs,
        in_specs=ins,
        out_specs=jax.tree.map(lambda _: VM, outs),
        scratch_shapes=scratch,
        compiler_params=PARAMS,
        name=name,
    )


def shape(*dims):
    return jax.ShapeDtypeStruct(dims, F32)


def shards(log_mean, tile_mask, coverage, lifetime, keep):
    rows, cols = log_mean.shape[1:]
    sections = keep.shape[0]
    parts = lax.axis_size("ta")
    share = cols // parts
    total = share + 2 * HALO
    used = rows * cols // LANES
    wide = -(-used // sections)
    padded = sections * wide

    sent = call(
        lambda *refs: prepare_body(wide, *refs),
        "prepare",
        shape(parts, total + 8, LANES),
        [VM] * 4,
        (pltpu.VMEM((cols + 2 * HALO, LANES), F32), pltpu.VMEM((cols, LANES), F32)),
    )(log_mean[0], tile_mask[0], coverage[0], lifetime)
    sent = lax.all_to_all(sent, "ta", 0, 0, tiled=True)

    place = np.arange(rows * parts)
    col_band = (np.abs(place[:, None] - place[None, :]) <= RADIUS).astype(BF16)
    offset = np.arange(total)[None, :] - np.arange(total - 2 * RADIUS)[:, None]
    row_band = ((offset >= 0) & (offset <= 2 * RADIUS)).astype(BF16)
    smoothed, rest, life = call(
        lambda *refs: smooth_body(wide, *refs),
        "smooth",
        (shape(padded, LANES), shape(used, LANES), shape(wide, LANES)),
        [VM] * 3,
    )(sent, col_band, row_band)

    def swap(values):
        flat = values.reshape(padded * LANES)
        flat = lax.all_to_all(flat, "gz", 0, 0, tiled=True)
        return flat.reshape(padded, LANES)

    long = shape(padded, LANES)
    fade, fore, back = call(
        norms_body, "norms", (shape(wide, LANES), long, long), [SM, VM]
    )(keep, life)
    drift = call(scan_body, "scan", long, [SM] + [VM] * 4)(
        keep, fade, fore, back, swap(smoothed)
    )
    out = call(finish_body, "finish", shape(share, rows * parts), [VM] * 2)(rest, swap(drift))
    return out.T[None]


def solution(mesh):
    return jax.shard_map(
        shards,
        mesh=mesh,
        in_specs=(
            P("gz", "ta", None),
            P("gz", "ta", None),
            P("gz", "ta", None),
            P("ta", None),
            P(),
        ),
        out_specs=P("gz", None, "ta"),
        check_vma=False,
    )
```

time: 90 us -> 84.7 us (0.941); the launches traced: 89.6 us -> 83 us
  starting transfers between devices: 32.6 us -> 14.4 us
  blocking collectives: 33 us -> 44.9 us
  waiting for transfers between devices: 13.4 us -> 12.3 us
    ppermute x2 -> x0, starting transfers between devices: 13.7 us -> none  [the longest x1 9.19 us: shards(): below = lax.ppermute(first, 'ta', down)]
    all_to_all x1, blocking collectives: 13.5 us -> 24.8 us  [shards(): sent = lax.all_to_all(sent, 'ta', 0, 0, tiled=True)]
    all_to_all x1, starting transfers between devices: 18.9 us -> 14.4 us  [swap(): flat = lax.all_to_all(flat, 'gz', 0, 0, tiled=True)]
    ppermute x2 -> x0, waiting for transfers between devices: 0.97 us -> none  [the longest x1 0.97 us: shards(): below = lax.ppermute(first, 'ta', down)]
    unnamed x10 -> x14, local copies, waits for them, and re-layouts: 3.34 us -> 4.28 us
    pallas_call x6 -> x5, Pallas kernels: 6.36 us -> 7.12 us  [the longest x1 4.48 us: shards(): call(lambda *refs: smooth_body(wide, *refs), 'smooth', (shape(padded, LAN...]
  transfers between devices with their start and end apart: 3 -> 1, of which waited for: 2 -> 1; matrix products, arithmetic and copies ran while one was open for 0% -> 0% of each run, Pallas kernels for 1% -> 1%
where the time goes in v3:
time: 84.7 us; the launch traced here: 83 us
  blocking collectives  44.9 us (53%)
  starting transfers between devices  14.4 us (17%)
  waiting for transfers between devices  12.3 us (15%)
  Pallas kernels  7.12 us (8%)
  local copies, waits for them, and re-layouts  4.28 us (5%)
    all_to_all x1, blocking collectives, shards(): sent = lax.all_to_all(sent, 'ta', 0, 0, tiled=True)  24.8 us
    all_to_all x1, blocking collectives, swap(): flat = lax.all_to_all(flat, 'gz', 0, 0, tiled=True)  20 us
    all_to_all x1, starting transfers between devices, swap(): flat = lax.all_to_all(flat, 'gz', 0, 0, tiled=True)  14.4 us
    all_to_all x1, waiting for transfers between devices, swap(): flat = lax.all_to_all(flat, 'gz', 0, 0, tiled=True)  12.3 us
    pallas_call x1, Pallas kernels, shards(): call(lambda *refs: smooth_body(wide, *refs), 'smooth', (shape(padded, LAN...  4.48 us
    unnamed x14, local copies, waits for them, and re-layouts  4.28 us
  transfers between devices with their start and end apart: 1, of which 1 were waited for; matrix products, arithmetic and copies ran while one was open for 0% of the time, Pallas kernels for 1%

profile of v3, /device:TPU:1, one launch (start us, length us, event | category | flops | bytes accessed | tf_op | source)
XLA Modules:
  0.0 83.0 jit_solution(13646864641981780246)
XLA Ops:
  0.0 0.0 copy-start.1
  0.0 0.9 %copy-done.1 = f32[1,64,512]{2,1,0:T(8,128)S(1)} copy-done((f32[1,64,512]{2,1,0:T(8,128)S(1)}, f32[1,64,512]{2,1,0:T(8,128)}, u32[]{:S(2)}) %copy-start.1) | copy-done | bytes 131096
  0.9 0.0 copy-start.2
  0.9 0.9 %copy-done.2 = s32[1,64,512]{2,1,0:T(8,128)S(1)} copy-done((s32[1,64,512]{2,1,0:T(8,128)S(1)}, s32[1,64,512]{2,1,0:T(8,128)}, u32[]{:S(2)}) %copy-start.2) | copy-done | bytes 131096
  1.8 0.0 copy-start.3
  1.8 0.9 %copy-done.3 = s32[1,64,512]{2,1,0:T(8,128)S(1)} copy-done((s32[1,64,512]{2,1,0:T(8,128)S(1)}, s32[1,64,512]{2,1,0:T(8,128)}, u32[]{:S(2)}) %copy-start.3) | copy-done | bytes 131096
  2.7 0.0 copy-start.4
  2.7 0.9 %copy-done.4 = f32[64,512]{1,0:T(8,128)S(1)} copy-done((f32[64,512]{1,0:T(8,128)S(1)}, f32[64,512]{1,0:T(8,128)}, u32[]{:S(2)}) %copy-start.4) | copy-done | bytes 131096
  3.6 0.2 prepare.1
  3.8 0.0 copy-start
  3.9 0.0 copy-start.5
  3.9 24.8 %all_to_all.23.refs_0_ = f32[8,184,128]{2,1,0:T(8,128)S(1)} all-to-all(f32[8,184,128]{2,1,0:T(8,128)S(1)} %prepare.1), channel_id=1, replica_groups=mesh['gz'=96,'ta'=8] {'ta'}, dimensions={0} | all-to-all | bytes 1507328 | tf_op jit(solution)/shard_map/all_to_all | solution.py:181
  28.7 0.0 copy-done
  28.7 0.0 copy-done.5
  28.7 4.5 %smooth.1 = (f32[288,128]{1,0:T(8,128)}, f32[256,128]{1,0:T(8,128)S(1)}, f32[3,128]{1,0:T(4,128)S(1)}) custom-call(f32[8,184,128]{2,1,0:T(8,128)S(1)} %all_to_all.23.refs_0_, bf16[512,512]{1,0:T(8,128)(2,1)S(1)} %copy-done, bf16[160,176]{1,0:T(8,128)(2,1)S(1)} %copy-done.5), custom_call_target="tpu_custom_call" | custom-call | tf_op jit(solution)/shard_map/smooth/pallas_call | solution.py:187
  33.2 14.4 %all-to-all-start.1 = ((f32[96,384,1]{1,2,0:T(1,128)}), f32[96,384,1]{1,2,0:T(1,128)S(1)}, u32[]{:S(2)}, u32[]{:S(2)}) async-start(f32[96,384,1]{1,2,0:T(1,128)} %bitcast.3), calls=%async_computation.1 | async-start | bytes 294912 | tf_op jit(solution)/shard_map/all_to_all | solution.py:196
  47.6 0.0 copy-start.6
  47.6 0.6 copy-done.6
  48.3 0.8 norms.1
  49.1 12.3 %all-to-all-done.1 = f32[96,384,1]{1,2,0:T(1,128)S(1)} async-done(((f32[96,384,1]{1,2,0:T(1,128)}), f32[96,384,1]{1,2,0:T(1,128)S(1)}, u32[]{:S(2)}, u32[]{:S(2)}) %all-to-all-start.1) | async-done | bytes 147488 | tf_op jit(solution)/shard_map/all_to_all | solution.py:196
  61.3 1.0 %scan.1 = f32[288,128]{1,0:T(8,128)S(1)} custom-call(f32[96]{0:T(128)S(1)} %copy-done.6, f32[3,128]{1,0:T(4,128)S(1)} %get-tuple-element.13.fade_ref, f32[288,128]{1,0:T(8,128)S(1)} %get-tuple-element.14.fore_ref, f32[288,128]{1,0:T(8,128)S(1)} %get-tuple-element.15.back_ref, f32[288,128]{1,0:T(8,128)S(1)} %bitcast.11), custom_call_target="tpu_custom_call" | custom-call | tf_op jit(solution)/shard_map/scan/pallas_call | solution.py:203
  62.3 20.0 %all_to_all.24 = f32[96,384,1]{1,2,0:T(1,128)S(1)} all-to-all(f32[96,384,1]{1,2,0:T(1,128)S(1)} %bitcast.12), channel_id=1, replica_groups=mesh['gz'=96,'ta'=8] {'gz'}, dimensions={0} | all-to-all | bytes 294912 | tf_op jit(solution)/shard_map/all_to_all | solution.py:196
  82.3 0.7 finish.1
Async XLA Ops:
  0.0 0.9 %copy-start.1 = (f32[1,64,512]{2,1,0:T(8,128)S(1)}, f32[1,64,512]{2,1,0:T(8,128)}, u32[]{:S(2)}) copy-start(f32[1,64,512]{2,1,0:T(8,128)} %param.7) | copy-start | bytes 393220
  0.9 0.9 %copy-start.2 = (s32[1,64,512]{2,1,0:T(8,128)S(1)}, s32[1,64,512]{2,1,0:T(8,128)}, u32[]{:S(2)}) copy-start(s32[1,64,512]{2,1,0:T(8,128)} %param.8) | copy-start | bytes 393220
  1.8 0.9 %copy-start.3 = (s32[1,64,512]{2,1,0:T(8,128)S(1)}, s32[1,64,512]{2,1,0:T(8,128)}, u32[]{:S(2)}) copy-start(s32[1,64,512]{2,1,0:T(8,128)} %param.9) | copy-start | bytes 393220
  2.7 0.9 %copy-start.4 = (f32[64,512]{1,0:T(8,128)S(1)}, f32[64,512]{1,0:T(8,128)}, u32[]{:S(2)}) copy-start(f32[64,512]{1,0:T(8,128)} %refs_3_.1) | copy-start | bytes 393220
  3.8 24.9 %copy-start = (bf16[512,512]{1,0:T(8,128)(2,1)S(1)}, bf16[512,512]{1,0:T(8,128)(2,1)}, u32[]{:S(2)}) copy-start(bf16[512,512]{1,0:T(8,128)(2,1)} %constant.4.clone.refs_1_) | copy-start | bytes 1572868
  3.9 24.9 %copy-start.5 = (bf16[160,176]{1,0:T(8,128)(2,1)S(1)}, bf16[160,176]{1,0:T(8,128)(2,1)}, u32[]{:S(2)}) copy-start(bf16[160,176]{1,0:T(8,128)(2,1)} %constant.5.clone.refs_2_) | copy-start | bytes 168964
  33.2 28.2 %all-to-all-start.1 = ((f32[96,384,1]{1,2,0:T(1,128)}), f32[96,384,1]{1,2,0:T(1,128)S(1)}, u32[]{:S(2)}, u32[]{:S(2)}) async-start(f32[96,384,1]{1,2,0:T(1,128)} %bitcast.3), calls=%async_computation.1 | async-start | bytes 294912 | tf_op jit(solution)/shard_map/all_to_all | solution.py:196
  47.6 0.7 copy-start.6

commit v4 on v3

--- a/solution.py
+++ b/solution.py
@@ -13,23 +13,35 @@
 F32 = jnp.float32
 BF16 = jnp.bfloat16
 VM = pl.BlockSpec(memory_space=pltpu.VMEM)
+HB = pl.BlockSpec(memory_space=pltpu.HBM)
 SM = pl.BlockSpec(memory_space=pltpu.SMEM)
 PARAMS = pltpu.CompilerParams(vmem_limit_bytes=16 << 20)
 
 
-def prepare_body(wide, log_ref, mask_ref, cov_ref, life_ref, out_ref, both_ref, life_t_ref):
+def prepare_body(
+    wide, log_hbm, mask_hbm, cov_hbm, life_hbm, out_ref,
+    log_ref, mask_ref, cov_ref, life_ref, both_ref, life_t_ref, sems,
+):
+    pairs = ((life_hbm, life_ref), (log_hbm, log_ref), (mask_hbm, mask_ref), (cov_hbm, cov_ref))
+    copies = [pltpu.make_async_copy(a, b, sems.at[i]) for i, (a, b) in enumerate(pairs)]
+    for copy in copies:
+        copy.start()
     rows, cols = log_ref.shape
     parts, depth, _ = out_ref.shape
     share = cols // parts
     span = share + 2 * HALO
+    both_ref[:HALO, :] = jnp.zeros((HALO, LANES), F32)
+    both_ref[HALO + cols:, :] = jnp.zeros((HALO, LANES), F32)
+    copies[0].wait()
+    life = jnp.concatenate([life_ref[...], life_ref[...]], axis=0)
+    for c in range(0, cols, LANES):
+        life_t_ref[c:c + LANES, :] = life[:, c:c + LANES].T
+    for copy in copies[1:]:
+        copy.wait()
     weight = 1.0 + mask_ref[...].astype(F32) * cov_ref[...].astype(F32)
     both = jnp.concatenate([weight, log_ref[...]], axis=0)
-    life = jnp.concatenate([life_ref[...], life_ref[...]], axis=0)
-    both_ref[:HALO, :] = jnp.zeros((HALO, LANES), F32)
-    both_ref[HALO + cols:, :] = jnp.zeros((HALO, LANES), F32)
     for c in range(0, cols, LANES):
         both_ref[HALO + c:HALO + c + LANES, :] = both[:, c:c + LANES].T
-        life_t_ref[c:c + LANES, :] = life[:, c:c + LANES].T
     first = lax.axis_index("gz") * wide
     for t in range(parts):
         out_ref[t, :span, :] = both_ref[share * t:share * t + span, :]
@@ -44,24 +56,55 @@
     return high, (values - high.astype(F32)).astype(BF16)
 
 
-def box(values, col_band, row_band):
-    high, low = halves(values)
-    cols = jnp.dot(high, col_band, preferred_element_type=F32) + jnp.dot(
-        low, col_band, preferred_element_type=F32
-    )
-    rows_in = values.shape[0]
-    rows_out = rows_in - 2 * RADIUS
-    band = row_band[:rows_out, :rows_in]
-    high, low = halves(cols)
-    return jnp.dot(band, high, preferred_element_type=F32) + jnp.dot(
-        band, low, preferred_element_type=F32
-    )
-
-
-def smooth_body(wide, in_ref, cb_ref, rb_ref, s_ref, e_ref, life_ref):
+def dot(a, b):
+    return jnp.dot(a, b, preferred_element_type=F32)
+
+
+def along_lanes(tiles, band, joint):
+    values = jnp.concatenate(tiles, axis=0)
+    rows = values.shape[0]
+    half = band.shape[0]
+    edge = half // 2
+    both = jnp.concatenate(halves(values), axis=0)
+    sides = dot(jnp.concatenate([both[:, :half], both[:, half:]], axis=0), band)
+    left, right = sides[:2 * rows], sides[2 * rows:]
+    across = dot(both[:, edge:half + edge], joint)
+    both = jnp.concatenate(
+        [
+            left[:, :edge],
+            left[:, edge:] + across[:, :edge],
+            right[:, :edge] + across[:, edge:],
+            right[:, edge:],
+        ],
+        axis=1,
+    )
+    sums = both[:rows] + both[rows:]
+    return [sums[r:r + 8] for r in range(0, rows, 8)]
+
+
+def along_rows(tiles):
+    count = len(tiles)
+    row = lax.broadcasted_iota(jnp.int32, tiles[0].shape, 0)
+    level = tiles
+    for k in (1, 2, 4):
+        turned = [pltpu.roll(v, 8 - k, 0) for v in level]
+        after = turned[1:] + turned[-1:]
+        level = [
+            v + jnp.where(row < 8 - k, a, b) for v, a, b in zip(level, turned, after)
+        ]
+    return [level[j] + level[j + 1] + tiles[j + 2] for j in range(count - 2)]
+
+
+def box(tiles, band, joint):
+    return along_rows(along_lanes(tiles, band, joint))
+
+
+def smooth_body(
+    wide, in_ref, band_ref, joint_ref, s_ref, e_ref, life_ref, inverse_ref, scale_ref
+):
     parts = in_ref.shape[0]
     half = LANES // 2
-    total = rb_ref.shape[1]
+    total = inverse_ref.shape[0] + 2 * RADIUS
     share = total - 2 * HALO
     left = lax.broadcasted_iota(jnp.int32, (total, LANES), 1) < half
     weights, fields = [], []
@@ -81,19 +124,22 @@
         b = in_ref[pair + 1, total + i:total + i + 1, :]
         life_ref[i:i + 1, :] = jnp.where(left, a, b)
 
-    col_band = cb_ref[...]
-    row_band = rb_ref[...]
-    denom = jnp.maximum(box(weight, col_band, row_band), 1.0)
-    inverse = 1.0 / denom
-    scale = weight[RADIUS:total - RADIUS] * inverse
-    now = weight * field
-    trim = 0
+    band = band_ref[...]
+    joint = joint_ref[...]
+    weights = [weight[r:r + 8] for r in range(0, total, 8)]
+    now = [w * field[8 * j:8 * j + 8] for j, w in enumerate(weights)]
+    denoms = box(weights, band, joint)
+    inverse = [1.0 / jnp.maximum(d, 1.0) for d in denoms]
+    for j, value in enumerate(inverse):
+        inverse_ref[8 * j:8 * j + 8, :] = value
+        scale_ref[8 * j:8 * j + 8, :] = value * weights[j + 1]
     for level in range(PASSES):
-        now = box(now, col_band, row_band)
-        if level < PASSES - 1:
-            now = now * scale[trim:scale.shape[0] - trim]
-            trim += RADIUS
-    smoothed = now * inverse[trim:inverse.shape[0] - trim]
+        now = box(now, band, joint)
+        factor = scale_ref if level < PASSES - 1 else inverse_ref
+        now = [
+            v * factor[8 * (j + level):8 * (j + level + 1), :] for j, v in enumerate(now)
+        ]
+    smoothed = jnp.concatenate(now, axis=0)
     rest = field[HALO:HALO + share] - smoothed
     for c in range(parts // 2):
         s_ref[c * share:(c + 1) * share, :] = smoothed[:, c * LANES:(c + 1) * LANES]
@@ -157,6 +203,10 @@
     )
 
 
+def in_hbm(values):
+    return pltpu.with_memory_space_constraint(values, pltpu.HBM)
+
+
 def shape(*dims):
     return jax.ShapeDtypeStruct(dims, F32)
 
@@ -175,21 +225,25 @@
         lambda *refs: prepare_body(wide, *refs),
         "prepare",
         shape(parts, total + 8, LANES),
-        [VM] * 4,
-        (pltpu.VMEM((cols + 2 * HALO, LANES), F32), pltpu.VMEM((cols, LANES), F32)),
-    )(log_mean[0], tile_mask[0], coverage[0], lifetime)
+        [HB] * 4,
+        [pltpu.VMEM((rows, cols), a.dtype) for a in (log_mean, tile_mask, coverage, lifetime)]
+        + [pltpu.VMEM((cols + 2 * HALO, LANES), F32), pltpu.VMEM((cols, LANES), F32)]
+        + [pltpu.SemaphoreType.DMA((4,))],
+    )(*(in_hbm(a) for a in (log_mean[0], tile_mask[0], coverage[0], lifetime)))
     sent = lax.all_to_all(sent, "ta", 0, 0, tiled=True)
 
-    place = np.arange(rows * parts)
-    col_band = (np.abs(place[:, None] - place[None, :]) <= RADIUS).astype(BF16)
-    offset = np.arange(total)[None, :] - np.arange(total - 2 * RADIUS)[:, None]
-    row_band = ((offset >= 0) & (offset <= 2 * RADIUS)).astype(BF16)
+    half = np.arange(rows * parts // 2)
+    near = np.abs(half[:, None] - half[None, :]) <= RADIUS
+    left = half < half.size // 2
+    band = near.astype(BF16)
+    joint = (near & (left[:, None] != left[None, :])).astype(BF16)
     smoothed, rest, life = call(
         lambda *refs: smooth_body(wide, *refs),
         "smooth",
         (shape(padded, LANES), shape(used, LANES), shape(wide, LANES)),
         [VM] * 3,
-    )(sent, col_band, row_band)
+        [pltpu.VMEM((total - 2 * RADIUS, rows * parts), F32)] * 2,
+    )(sent, band, joint)
 
     def swap(values):
         flat = values.reshape(padded * LANES)

time: 84.7 us -> 80.3 us (0.948)
  the two profiles are of different devices: /device:TPU:1 before, /device:TPU:8 now
where the time goes in v4:
time: 80.3 us; the launch traced here: 80 us
  blocking collectives  37.4 us (47%)
  starting transfers between devices  21.8 us (27%)
  waiting for transfers between devices  13.8 us (17%)
  Pallas kernels  6.38 us (8%)
    all_to_all x1, starting transfers between devices, swap(): flat = lax.all_to_all(flat, 'gz', 0, 0, tiled=True)  21.8 us
    all_to_all x1, blocking collectives, swap(): flat = lax.all_to_all(flat, 'gz', 0, 0, tiled=True)  20.3 us
    all_to_all x1, blocking collectives, shards(): sent = lax.all_to_all(sent, 'ta', 0, 0, tiled=True)  17 us
    all_to_all x1, waiting for transfers between devices, swap(): flat = lax.all_to_all(flat, 'gz', 0, 0, tiled=True)  13.8 us
    pallas_call x1, Pallas kernels, shards(): call(lambda *refs: smooth_body(wide, *refs), 'smooth', (shape(padded, LAN...  2.7 us
  transfers between devices with their start and end apart: 1, of which 1 were waited for; matrix products, arithmetic and copies ran while one was open for 0% of the time, Pallas kernels for 1%

profile of v4, /device:TPU:8, one launch (start us, length us, event | category | flops | bytes accessed | tf_op | source)
XLA Modules:
  0.0 80.0 jit_solution(14219693546539909405)
XLA Ops:
  0.0 1.3 %prepare.1 = f32[8,184,128]{2,1,0:T(8,128)S(1)} custom-call(f32[64,512]{1,0:T(8,128)} %bitcast.13, s32[64,512]{1,0:T(8,128)} %bitcast.14, s32[64,512]{1,0:T(8,128)} %bitcast.15, f32[64,512]{1,0:T(8,128)} %refs_3_.1), custom_call_target="tpu_custom_call" | custom-call | tf_op jit(solution)/shard_map/prepare/pallas_call | solution.py:224
  1.3 0.0 copy-start
  1.3 0.0 copy-start.1
  1.3 17.0 %all_to_all.23.refs_0_ = f32[8,184,128]{2,1,0:T(8,128)S(1)} all-to-all(f32[8,184,128]{2,1,0:T(8,128)S(1)} %prepare.1), channel_id=1, replica_groups=mesh['gz'=96,'ta'=8] {'ta'}, dimensions={0} | all-to-all | bytes 1507328 | tf_op jit(solution)/shard_map/all_to_all | solution.py:233
  18.3 0.0 copy-done
  18.3 0.0 copy-done.1
  18.3 2.7 %smooth.1 = (f32[288,128]{1,0:T(8,128)}, f32[256,128]{1,0:T(8,128)S(1)}, f32[3,128]{1,0:T(4,128)S(1)}) custom-call(f32[8,184,128]{2,1,0:T(8,128)S(1)} %all_to_all.23.refs_0_, bf16[256,256]{1,0:T(8,128)(2,1)S(1)} %copy-done.1, bf16[256,256]{1,0:T(8,128)(2,1)S(1)} %copy-done), custom_call_target="tpu_custom_call" | custom-call | tf_op jit(solution)/shard_map/smooth/pallas_call | solution.py:240
  21.0 21.8 %all-to-all-start.1 = ((f32[96,384,1]{1,2,0:T(1,128)}), f32[96,384,1]{1,2,0:T(1,128)S(1)}, u32[]{:S(2)}, u32[]{:S(2)}) async-start(f32[96,384,1]{1,2,0:T(1,128)} %bitcast.3), calls=%async_computation.1 | async-start | bytes 294912 | tf_op jit(solution)/shard_map/all_to_all | solution.py:250
  42.8 0.0 copy-start.2
  42.8 0.6 copy-done.2
  43.5 0.8 norms.1
  44.3 13.8 %all-to-all-done.1 = f32[96,384,1]{1,2,0:T(1,128)S(1)} async-done(((f32[96,384,1]{1,2,0:T(1,128)}), f32[96,384,1]{1,2,0:T(1,128)S(1)}, u32[]{:S(2)}, u32[]{:S(2)}) %all-to-all-start.1) | async-done | bytes 147488 | tf_op jit(solution)/shard_map/all_to_all | solution.py:250
  58.1 1.0 %scan.1 = f32[288,128]{1,0:T(8,128)S(1)} custom-call(f32[96]{0:T(128)S(1)} %copy-done.2, f32[3,128]{1,0:T(4,128)S(1)} %get-tuple-element.13.fade_ref, f32[288,128]{1,0:T(8,128)S(1)} %get-tuple-element.14.fore_ref, f32[288,128]{1,0:T(8,128)S(1)} %get-tuple-element.15.back_ref, f32[288,128]{1,0:T(8,128)S(1)} %bitcast.11), custom_call_target="tpu_custom_call" | custom-call | tf_op jit(solution)/shard_map/scan/pallas_call | solution.py:257
  59.0 20.3 %all_to_all.24 = f32[96,384,1]{1,2,0:T(1,128)S(1)} all-to-all(f32[96,384,1]{1,2,0:T(1,128)S(1)} %bitcast.12), channel_id=1, replica_groups=mesh['gz'=96,'ta'=8] {'gz'}, dimensions={0} | all-to-all | bytes 294912 | tf_op jit(solution)/shard_map/all_to_all | solution.py:250
  79.3 0.7 finish.1
Async XLA Ops:
  1.3 17.1 %copy-start = (bf16[256,256]{1,0:T(8,128)(2,1)S(1)}, bf16[256,256]{1,0:T(8,128)(2,1)}, u32[]{:S(2)}) copy-start(bf16[256,256]{1,0:T(8,128)(2,1)} %constant.5.clone.refs_2_) | copy-start | bytes 393220
  1.3 17.1 %copy-start.1 = (bf16[256,256]{1,0:T(8,128)(2,1)S(1)}, bf16[256,256]{1,0:T(8,128)(2,1)}, u32[]{:S(2)}) copy-start(bf16[256,256]{1,0:T(8,128)(2,1)} %constant.4.clone.refs_1_) | copy-start | bytes 393220
  21.0 37.0 %all-to-all-start.1 = ((f32[96,384,1]{1,2,0:T(1,128)}), f32[96,384,1]{1,2,0:T(1,128)S(1)}, u32[]{:S(2)}, u32[]{:S(2)}) async-start(f32[96,384,1]{1,2,0:T(1,128)} %bitcast.3), calls=%async_computation.1 | async-start | bytes 294912 | tf_op jit(solution)/shard_map/all_to_all | solution.py:250
  42.8 0.7 copy-start.2

commit v5 on v4

--- a/solution.py
+++ b/solution.py
@@ -9,6 +9,7 @@
 RADIUS = 8
 PASSES = 7
 HALO = RADIUS * PASSES
+START = 67
 LANES = 128
 F32 = jnp.float32
 BF16 = jnp.bfloat16
@@ -19,7 +20,7 @@
 
 
 def prepare_body(
-    wide, log_hbm, mask_hbm, cov_hbm, life_hbm, out_ref,
+    wide, turn, log_hbm, mask_hbm, cov_hbm, life_hbm, out_ref,
     log_ref, mask_ref, cov_ref, life_ref, both_ref, life_t_ref, sems,
 ):
     pairs = ((life_hbm, life_ref), (log_hbm, log_ref), (mask_hbm, mask_ref), (cov_hbm, cov_ref))
@@ -42,7 +43,8 @@
     both = jnp.concatenate([weight, log_ref[...]], axis=0)
     for c in range(0, cols, LANES):
         both_ref[HALO + c:HALO + c + LANES, :] = both[:, c:c + LANES].T
-    first = lax.axis_index("gz") * wide
+    sections = lax.axis_size("gz")
+    first = lax.rem(lax.axis_index("gz") + sections - turn, sections) * wide
     for t in range(parts):
         out_ref[t, :span, :] = both_ref[share * t:share * t + span, :]
         out_ref[t, span:, :] = jnp.zeros((depth - span, LANES), F32)
@@ -100,7 +102,7 @@
 
 
 def smooth_body(
-    wide, in_ref, band_ref, joint_ref, s_ref, e_ref, life_ref, inverse_ref, scale_ref
+    wide, turn, in_ref, band_ref, joint_ref, s_ref, e_ref, life_ref, inverse_ref, scale_ref
 ):
     parts = in_ref.shape[0]
     half = LANES // 2
@@ -116,7 +118,8 @@
     weight = jnp.concatenate(weights, axis=1)
     field = jnp.concatenate(fields, axis=1)
 
-    first = lax.axis_index("gz") * wide
+    sections = lax.axis_size("gz")
+    first = lax.rem(lax.axis_index("gz") + sections - turn, sections) * wide
     left = lax.broadcasted_iota(jnp.int32, (1, LANES), 1) < half
     for i in range(wide):
         pair = 2 * jnp.minimum((first + i) // share, parts // 2 - 1)
@@ -166,22 +169,26 @@
         back_ref[z * wide:(z + 1) * wide, :] = 1.0 / norm
 
 
-def scan_body(keep_ref, fade_ref, fore_ref, back_ref, s_ref, out_ref):
+def scan_body(turn, keep_ref, fade_ref, fore_ref, back_ref, s_ref, out_ref):
     sections = keep_ref.shape[0]
     wide = fade_ref.shape[0]
     fade = fade_ref[...]
     mass = jnp.zeros_like(fade)
+
+    def rows(z):
+        return slice(z * wide, (z + 1) * wide)
+
     for z in range(sections):
         decay = keep_ref[z] * fade
-        at = slice(z * wide, (z + 1) * wide)
+        at = rows((z - turn) % sections)
         mass = decay * mass + (1.0 - decay) * s_ref[at, :]
-        out_ref[at, :] = mass * fore_ref[at, :]
+        out_ref[at, :] = mass * fore_ref[rows(z), :]
     mass = jnp.zeros_like(fade)
     for z in reversed(range(sections)):
         decay = keep_ref[z] * fade
-        at = slice(z * wide, (z + 1) * wide)
+        at = rows((z - turn) % sections)
         mass = decay * mass + out_ref[at, :]
-        out_ref[at, :] = mass * back_ref[at, :]
+        out_ref[at, :] = mass * back_ref[rows(z), :]
 
 
 def finish_body(e_ref, drift_ref, out_ref):
@@ -220,9 +227,10 @@
     used = rows * cols // LANES
     wide = -(-used // sections)
     padded = sections * wide
+    turn = START % sections
 
     sent = call(
-        lambda *refs: prepare_body(wide, *refs),
+        lambda *refs: prepare_body(wide, turn, *refs),
         "prepare",
         shape(parts, total + 8, LANES),
         [HB] * 4,
@@ -238,23 +246,25 @@
     band = near.astype(BF16)
     joint = (near & (left[:, None] != left[None, :])).astype(BF16)
     smoothed, rest, life = call(
-        lambda *refs: smooth_body(wide, *refs),
+        lambda *refs: smooth_body(wide, turn, *refs),
         "smooth",
         (shape(padded, LANES), shape(used, LANES), shape(wide, LANES)),
         [VM] * 3,
         [pltpu.VMEM((total - 2 * RADIUS, rows * parts), F32)] * 2,
     )(sent, band, joint)
 
+    order = [(i + turn) % sections for i in range(sections)]
+
     def swap(values):
         flat = values.reshape(padded * LANES)
-        flat = lax.all_to_all(flat, "gz", 0, 0, tiled=True)
+        flat = lax.all_to_all(flat, "gz", 0, 0, tiled=True, axis_index_groups=[order])
         return flat.reshape(padded, LANES)
 
     long = shape(padded, LANES)
     fade, fore, back = call(
         norms_body, "norms", (shape(wide, LANES), long, long), [SM, VM]
     )(keep, life)
-    drift = call(scan_body, "scan", long, [SM] + [VM] * 4)(
+    drift = call(lambda *refs: scan_body(turn, *refs), "scan", long, [SM] + [VM] * 4)(
         keep, fade, fore, back, swap(smoothed)
     )
     out = call(finish_body, "finish", shape(share, rows * parts), [VM] * 2)(rest, swap(drift))

time: 80.3 us -> 74.3 us (0.925)
  the two profiles are of different devices: /device:TPU:8 before, /device:TPU:1 now
where the time goes in v5:
time: 74.3 us; the launch traced here: 73.4 us
  blocking collectives  44.6 us (60%)
  starting transfers between devices  17.7 us (24%)
  Pallas kernels  6.38 us (9%)
  waiting for transfers between devices  3.97 us (5%)
    all_to_all x1, blocking collectives, shards(): sent = lax.all_to_all(sent, 'ta', 0, 0, tiled=True)  24.8 us
    all_to_all x1, blocking collectives, swap(): lax.all_to_all(flat, 'gz', 0, 0, tiled=True, axis_index_groups=[order])  19.8 us
    all_to_all x1, starting transfers between devices, swap(): lax.all_to_all(flat, 'gz', 0, 0, tiled=True, axis_index_groups=[order])  17.7 us
    all_to_all x1, waiting for transfers between devices, swap(): lax.all_to_all(flat, 'gz', 0, 0, tiled=True, axis_index_groups=[order])  3.97 us
    pallas_call x1, Pallas kernels, shards(): call(lambda *refs: smooth_body(wide, turn, *refs), 'smooth', (shape(padde...  2.68 us
  transfers between devices with their start and end apart: 1, of which 1 were waited for; matrix products, arithmetic and copies ran while one was open for 0% of the time, Pallas kernels for 1%

profile of v5, /device:TPU:1, one launch (start us, length us, event | category | flops | bytes accessed | tf_op | source)
XLA Modules:
  0.0 73.4 jit_solution(18108427079004429625)
XLA Ops:
  0.0 1.3 %prepare.1 = f32[8,184,128]{2,1,0:T(8,128)S(1)} custom-call(f32[64,512]{1,0:T(8,128)} %bitcast.13, s32[64,512]{1,0:T(8,128)} %bitcast.14, s32[64,512]{1,0:T(8,128)} %bitcast.15, f32[64,512]{1,0:T(8,128)} %refs_3_.1), custom_call_target="tpu_custom_call" | custom-call | tf_op jit(solution)/shard_map/prepare/pallas_call | solution.py:232
  1.3 0.0 copy-start
  1.3 0.0 copy-start.1
  1.3 24.8 %all_to_all.23.refs_0_ = f32[8,184,128]{2,1,0:T(8,128)S(1)} all-to-all(f32[8,184,128]{2,1,0:T(8,128)S(1)} %prepare.1), channel_id=1, replica_groups=mesh['gz'=96,'ta'=8] {'ta'}, dimensions={0} | all-to-all | bytes 1507328 | tf_op jit(solution)/shard_map/all_to_all | solution.py:241
  26.1 0.0 copy-done
  26.1 0.0 copy-done.1
  26.1 2.7 %smooth.1 = (f32[288,128]{1,0:T(8,128)}, f32[256,128]{1,0:T(8,128)S(1)}, f32[3,128]{1,0:T(4,128)S(1)}) custom-call(f32[8,184,128]{2,1,0:T(8,128)S(1)} %all_to_all.23.refs_0_, bf16[256,256]{1,0:T(8,128)(2,1)S(1)} %copy-done.1, bf16[256,256]{1,0:T(8,128)(2,1)S(1)} %copy-done), custom_call_target="tpu_custom_call" | custom-call | tf_op jit(solution)/shard_map/smooth/pallas_call | solution.py:248
  28.8 17.7 %all-to-all-start.1 = ((f32[96,384,1]{1,2,0:T(1,128)}), f32[96,384,1]{1,2,0:T(1,128)S(1)}, u32[]{:S(2)}, u32[]{:S(2)}) async-start(f32[96,384,1]{1,2,0:T(1,128)} %bitcast.3), calls=%async_computation.1 | async-start | bytes 294912 | tf_op jit(solution)/shard_map/all_to_all | solution.py:260
  46.6 0.0 copy-start.2
  46.6 0.6 copy-done.2
  47.2 0.8 %norms.1 = (f32[3,128]{1,0:T(4,128)S(1)}, f32[288,128]{1,0:T(8,128)S(1)}, f32[288,128]{1,0:T(8,128)S(1)}) custom-call(f32[96]{0:T(128)S(1)} %copy-done.2, f32[3,128]{1,0:T(4,128)S(1)} %get-tuple-element.12.life_ref), custom_call_target="tpu_custom_call" | custom-call | tf_op jit(solution)/shard_map/norms/pallas_call | solution.py:264
  48.0 4.0 %all-to-all-done.1 = f32[96,384,1]{1,2,0:T(1,128)S(1)} async-done(((f32[96,384,1]{1,2,0:T(1,128)}), f32[96,384,1]{1,2,0:T(1,128)S(1)}, u32[]{:S(2)}, u32[]{:S(2)}) %all-to-all-start.1) | async-done | bytes 147488 | tf_op jit(solution)/shard_map/all_to_all | solution.py:260
  52.0 1.0 %scan.1 = f32[288,128]{1,0:T(8,128)S(1)} custom-call(f32[96]{0:T(128)S(1)} %copy-done.2, f32[3,128]{1,0:T(4,128)S(1)} %get-tuple-element.13.refs_1_, f32[288,128]{1,0:T(8,128)S(1)} %get-tuple-element.14.refs_2_, f32[288,128]{1,0:T(8,128)S(1)} %get-tuple-element.15.refs_3_, f32[288,128]{1,0:T(8,128)S(1)} %bitcast.11), custom_call_target="tpu_custom_call" | custom-call | tf_op jit(solution)/shard_map/scan/pallas_call | solution.py:267
  53.0 19.8 %all_to_all.24 = f32[96,384,1]{1,2,0:T(1,128)S(1)} all-to-all(f32[96,384,1]{1,2,0:T(1,128)S(1)} %bitcast.12), channel_id=1, replica_groups={{536,544,552,560,568,576,584,592,600,608,616,624,632,640,648,656,664,67..., dimensions={0} | all-to-all | bytes 294912 | tf_op jit(solution)/shard_map/all_to_all | solution.py:260
  72.7 0.7 finish.1
Async XLA Ops:
  1.3 24.9 %copy-start = (bf16[256,256]{1,0:T(8,128)(2,1)S(1)}, bf16[256,256]{1,0:T(8,128)(2,1)}, u32[]{:S(2)}) copy-start(bf16[256,256]{1,0:T(8,128)(2,1)} %constant.5.clone.refs_2_) | copy-start | bytes 393220
  1.3 24.9 %copy-start.1 = (bf16[256,256]{1,0:T(8,128)(2,1)S(1)}, bf16[256,256]{1,0:T(8,128)(2,1)}, u32[]{:S(2)}) copy-start(bf16[256,256]{1,0:T(8,128)(2,1)} %constant.4.clone.refs_1_) | copy-start | bytes 393220
  28.8 23.2 %all-to-all-start.1 = ((f32[96,384,1]{1,2,0:T(1,128)}), f32[96,384,1]{1,2,0:T(1,128)S(1)}, u32[]{:S(2)}, u32[]{:S(2)}) async-start(f32[96,384,1]{1,2,0:T(1,128)} %bitcast.3), calls=%async_computation.1 | async-start | bytes 294912 | tf_op jit(solution)/shard_map/all_to_all | solution.py:260
  46.6 0.7 copy-start.2

commit v6 on v5

--- a/solution.py
+++ b/solution.py
@@ -10,6 +10,7 @@
 PASSES = 7
 HALO = RADIUS * PASSES
 START = 67
+FIRST = 7
 LANES = 128
 F32 = jnp.float32
 BF16 = jnp.bfloat16
@@ -46,11 +47,12 @@
     sections = lax.axis_size("gz")
     first = lax.rem(lax.axis_index("gz") + sections - turn, sections) * wide
     for t in range(parts):
-        out_ref[t, :span, :] = both_ref[share * t:share * t + span, :]
-        out_ref[t, span:, :] = jnp.zeros((depth - span, LANES), F32)
+        slot = (t - FIRST) % parts
+        out_ref[slot, :span, :] = both_ref[share * t:share * t + span, :]
+        out_ref[slot, span:, :] = jnp.zeros((depth - span, LANES), F32)
         for i in range(wide):
             place = share * t + (first + i) % share
-            out_ref[t, span + i:span + i + 1, :] = life_t_ref[pl.ds(place, 1), :]
+            out_ref[slot, span + i:span + i + 1, :] = life_t_ref[pl.ds(place, 1), :]
 
 
 def halves(values):
@@ -111,8 +113,8 @@
     left = lax.broadcasted_iota(jnp.int32, (total, LANES), 1) < half
     weights, fields = [], []
     for t in range(0, parts, 2):
-        a = in_ref[t, :total, :]
-        b = in_ref[t + 1, :total, :]
+        a = in_ref[(t - FIRST) % parts, :total, :]
+        b = in_ref[(t + 1 - FIRST) % parts, :total, :]
         weights.append(jnp.where(left, a, pltpu.roll(b, half, 1)))
         fields.append(jnp.where(left, pltpu.roll(a, half, 1), b))
     weight = jnp.concatenate(weights, axis=1)
@@ -123,8 +125,9 @@
     left = lax.broadcasted_iota(jnp.int32, (1, LANES), 1) < half
     for i in range(wide):
         pair = 2 * jnp.minimum((first + i) // share, parts // 2 - 1)
-        a = in_ref[pair, total + i:total + i + 1, :]
-        b = in_ref[pair + 1, total + i:total + i + 1, :]
+        shift = parts - FIRST
+        a = in_ref[lax.rem(pair + shift, parts), total + i:total + i + 1, :]
+        b = in_ref[lax.rem(pair + 1 + shift, parts), total + i:total + i + 1, :]
         life_ref[i:i + 1, :] = jnp.where(left, a, b)
 
     band = band_ref[...]
@@ -180,9 +183,8 @@
 
     for z in range(sections):
         decay = keep_ref[z] * fade
-        at = rows((z - turn) % sections)
-        mass = decay * mass + (1.0 - decay) * s_ref[at, :]
-        out_ref[at, :] = mass * fore_ref[rows(z), :]
+        mass = decay * mass + (1.0 - decay) * s_ref[rows((z - turn) % sections), :]
+        out_ref[rows((z - turn) % sections), :] = mass * fore_ref[rows(z), :]
     mass = jnp.zeros_like(fade)
     for z in reversed(range(sections)):
         decay = keep_ref[z] * fade
@@ -238,7 +240,8 @@
         + [pltpu.VMEM((cols + 2 * HALO, LANES), F32), pltpu.VMEM((cols, LANES), F32)]
         + [pltpu.SemaphoreType.DMA((4,))],
     )(*(in_hbm(a) for a in (log_mean[0], tile_mask[0], coverage[0], lifetime)))
-    sent = lax.all_to_all(sent, "ta", 0, 0, tiled=True)
+    ring = [(i + FIRST) % parts for i in range(parts)]
+    sent = lax.all_to_all(sent, "ta", 0, 0, tiled=True, axis_index_groups=[ring])
 
     half = np.arange(rows * parts // 2)
     near = np.abs(half[:, None] - half[None, :]) <= RADIUS

time: 74.3 us -> 73.1 us (0.984)
    all_to_all x1, starting transfers between devices: 17.7 us -> 17 us  [swap(): lax.all_to_all(flat, 'gz', 0, 0, tiled=True, axis_index_groups=[order])]
where the time goes in v6:
time: 73.1 us; the launch traced here: 72.2 us
  blocking collectives  44.1 us (60%)
  starting transfers between devices  17 us (23%)
  Pallas kernels  6.38 us (9%)
  waiting for transfers between devices  3.97 us (5%)
    all_to_all x1, blocking collectives, shards(): lax.all_to_all(sent, 'ta', 0, 0, tiled=True, axis_index_groups=[ring])  24.4 us
    all_to_all x1, blocking collectives, swap(): lax.all_to_all(flat, 'gz', 0, 0, tiled=True, axis_index_groups=[order])  19.8 us
    all_to_all x1, starting transfers between devices, swap(): lax.all_to_all(flat, 'gz', 0, 0, tiled=True, axis_index_groups=[order])  17 us
    all_to_all x1, waiting for transfers between devices, swap(): lax.all_to_all(flat, 'gz', 0, 0, tiled=True, axis_index_groups=[order])  3.97 us
    pallas_call x1, Pallas kernels, shards(): call(lambda *refs: smooth_body(wide, turn, *refs), 'smooth', (shape(padde...  2.68 us
  transfers between devices with their start and end apart: 1, of which 1 were waited for; matrix products, arithmetic and copies ran while one was open for 0% of the time, Pallas kernels for 1%

profile of v6, /device:TPU:1, one launch (start us, length us, event | category | flops | bytes accessed | tf_op | source)
XLA Modules:
  0.0 72.2 jit_solution(5475948166298122470)
XLA Ops:
  0.0 1.3 %prepare.1 = f32[8,184,128]{2,1,0:T(8,128)S(1)} custom-call(f32[64,512]{1,0:T(8,128)} %bitcast.13, s32[64,512]{1,0:T(8,128)} %bitcast.14, s32[64,512]{1,0:T(8,128)} %bitcast.15, f32[64,512]{1,0:T(8,128)} %refs_3_.1), custom_call_target="tpu_custom_call" | custom-call | tf_op jit(solution)/shard_map/prepare/pallas_call | solution.py:234
  1.3 0.0 copy-start
  1.3 0.0 copy-start.1
  1.3 24.4 %all_to_all.23.refs_0_ = f32[8,184,128]{2,1,0:T(8,128)S(1)} all-to-all(f32[8,184,128]{2,1,0:T(8,128)S(1)} %prepare.1), channel_id=1, replica_groups={{7,0,1,2,3,4,5,6},{15,8,9,10,11,12,13,14},{23,16,17,18,19,20,21,22},{31..., dimensions={0} | all-to-all | bytes 1507328 | tf_op jit(solution)/shard_map/all_to_all | solution.py:244
  25.7 0.0 copy-done
  25.7 0.0 copy-done.1
  25.7 2.7 %smooth.1 = (f32[288,128]{1,0:T(8,128)}, f32[256,128]{1,0:T(8,128)S(1)}, f32[3,128]{1,0:T(4,128)S(1)}) custom-call(f32[8,184,128]{2,1,0:T(8,128)S(1)} %all_to_all.23.refs_0_, bf16[256,256]{1,0:T(8,128)(2,1)S(1)} %copy-done.1, bf16[256,256]{1,0:T(8,128)(2,1)S(1)} %copy-done), custom_call_target="tpu_custom_call" | custom-call | tf_op jit(solution)/shard_map/smooth/pallas_call | solution.py:251
  28.4 17.0 %all-to-all-start.1 = ((f32[96,384,1]{1,2,0:T(1,128)}), f32[96,384,1]{1,2,0:T(1,128)S(1)}, u32[]{:S(2)}, u32[]{:S(2)}) async-start(f32[96,384,1]{1,2,0:T(1,128)} %bitcast.3), calls=%async_computation.1 | async-start | bytes 294912 | tf_op jit(solution)/shard_map/all_to_all | solution.py:263
  45.4 0.0 copy-start.2
  45.4 0.6 copy-done.2
  46.0 0.8 %norms.1 = (f32[3,128]{1,0:T(4,128)S(1)}, f32[288,128]{1,0:T(8,128)S(1)}, f32[288,128]{1,0:T(8,128)S(1)}) custom-call(f32[96]{0:T(128)S(1)} %copy-done.2, f32[3,128]{1,0:T(4,128)S(1)} %get-tuple-element.12.life_ref), custom_call_target="tpu_custom_call" | custom-call | tf_op jit(solution)/shard_map/norms/pallas_call | solution.py:267
  46.8 4.0 %all-to-all-done.1 = f32[96,384,1]{1,2,0:T(1,128)S(1)} async-done(((f32[96,384,1]{1,2,0:T(1,128)}), f32[96,384,1]{1,2,0:T(1,128)S(1)}, u32[]{:S(2)}, u32[]{:S(2)}) %all-to-all-start.1) | async-done | bytes 147488 | tf_op jit(solution)/shard_map/all_to_all | solution.py:263
  50.8 1.0 %scan.1 = f32[288,128]{1,0:T(8,128)S(1)} custom-call(f32[96]{0:T(128)S(1)} %copy-done.2, f32[3,128]{1,0:T(4,128)S(1)} %get-tuple-element.13.refs_1_, f32[288,128]{1,0:T(8,128)S(1)} %get-tuple-element.14.refs_2_, f32[288,128]{1,0:T(8,128)S(1)} %get-tuple-element.15.refs_3_, f32[288,128]{1,0:T(8,128)S(1)} %bitcast.11), custom_call_target="tpu_custom_call" | custom-call | tf_op jit(solution)/shard_map/scan/pallas_call | solution.py:270
  51.8 19.8 %all_to_all.24 = f32[96,384,1]{1,2,0:T(1,128)S(1)} all-to-all(f32[96,384,1]{1,2,0:T(1,128)S(1)} %bitcast.12), channel_id=1, replica_groups={{536,544,552,560,568,576,584,592,600,608,616,624,632,640,648,656,664,67..., dimensions={0} | all-to-all | bytes 294912 | tf_op jit(solution)/shard_map/all_to_all | solution.py:263
  71.5 0.7 finish.1
Async XLA Ops:
  1.3 24.4 %copy-start = (bf16[256,256]{1,0:T(8,128)(2,1)S(1)}, bf16[256,256]{1,0:T(8,128)(2,1)}, u32[]{:S(2)}) copy-start(bf16[256,256]{1,0:T(8,128)(2,1)} %constant.5.clone.refs_2_) | copy-start | bytes 393220
  1.3 24.4 %copy-start.1 = (bf16[256,256]{1,0:T(8,128)(2,1)S(1)}, bf16[256,256]{1,0:T(8,128)(2,1)}, u32[]{:S(2)}) copy-start(bf16[256,256]{1,0:T(8,128)(2,1)} %constant.4.clone.refs_1_) | copy-start | bytes 393220
  28.4 22.4 %all-to-all-start.1 = ((f32[96,384,1]{1,2,0:T(1,128)}), f32[96,384,1]{1,2,0:T(1,128)S(1)}, u32[]{:S(2)}, u32[]{:S(2)}) async-start(f32[96,384,1]{1,2,0:T(1,128)} %bitcast.3), calls=%async_computation.1 | async-start | bytes 294912 | tf_op jit(solution)/shard_map/all_to_all | solution.py:263
  45.4 0.7 copy-start.2

commit v7 on v6

--- a/solution.py
+++ b/solution.py
@@ -11,6 +11,7 @@
 HALO = RADIUS * PASSES
 START = 67
 FIRST = 7
+SPANS = 4
 LANES = 128
 F32 = jnp.float32
 BF16 = jnp.bfloat16
@@ -71,9 +72,12 @@
     edge = half // 2
     both = jnp.concatenate(halves(values), axis=0)
     sides = dot(jnp.concatenate([both[:, :half], both[:, half:]], axis=0), band)
-    left, right = sides[:2 * rows], sides[2 * rows:]
-    across = dot(both[:, edge:half + edge], joint)
-    both = jnp.concatenate(
+    left = sides[:rows] + sides[rows:2 * rows]
+    right = sides[2 * rows:3 * rows] + sides[3 * rows:]
+    near = lax.broadcasted_iota(jnp.int32, (rows, edge), 1) < edge // 2
+    middle = jnp.where(near, values[:, half:half + edge], values[:, edge:half])
+    across = dot(jnp.concatenate(halves(middle), axis=1), joint)
+    sums = jnp.concatenate(
         [
             left[:, :edge],
             left[:, edge:] + across[:, :edge],
@@ -82,7 +86,6 @@
         ],
         axis=1,
     )
-    sums = both[:rows] + both[rows:]
     return [sums[r:r + 8] for r in range(0, rows, 8)]
 
 
@@ -97,10 +100,6 @@
             v + jnp.where(row < 8 - k, a, b) for v, a, b in zip(level, turned, after)
         ]
     return [level[j] + level[j + 1] + tiles[j + 2] for j in range(count - 2)]
-
-
-def box(tiles, band, joint):
-    return along_rows(along_lanes(tiles, band, joint))
 
 
 def smooth_body(
@@ -134,13 +133,13 @@
     joint = joint_ref[...]
     weights = [weight[r:r + 8] for r in range(0, total, 8)]
     now = [w * field[8 * j:8 * j + 8] for j, w in enumerate(weights)]
-    denoms = box(weights, band, joint)
+    denoms = along_rows(along_lanes(weights, band, joint))
     inverse = [1.0 / jnp.maximum(d, 1.0) for d in denoms]
     for j, value in enumerate(inverse):
         inverse_ref[8 * j:8 * j + 8, :] = value
         scale_ref[8 * j:8 * j + 8, :] = value * weights[j + 1]
     for level in range(PASSES):
-        now = box(now, band, joint)
+        now = along_rows(along_lanes(now, band, joint))
         factor = scale_ref if level < PASSES - 1 else inverse_ref
         now = [
             v * factor[8 * (j + level):8 * (j + level + 1), :] for j, v in enumerate(now)
@@ -154,43 +153,80 @@
     s_ref[used:, :] = jnp.zeros((s_ref.shape[0] - used, LANES), F32)
 
 
-def norms_body(keep_ref, life_ref, fade_ref, fore_ref, back_ref):
+def norms_body(
+    keep_ref, life_ref, fade_ref, fore_ref, back_ref, fore_lead_ref, back_lead_ref, ends_ref
+):
     sections = keep_ref.shape[0]
     wide = life_ref.shape[0]
+    run = sections // SPANS
     fade = jnp.exp(-life_ref[...] / sections)
     fade_ref[...] = fade
     norm = jnp.zeros_like(fade)
+    lead = jnp.ones_like(fade)
     for z in range(sections):
+        at = slice(z * wide, (z + 1) * wide)
         decay = keep_ref[z] * fade
         gain = 1.0 - decay
         norm = decay * norm + gain
-        fore_ref[z * wide:(z + 1) * wide, :] = gain / norm
+        lead = lead * decay if z % run else decay
+        share = gain / norm
+        fore_ref[at, :] = share
+        fore_lead_ref[at, :] = lead * share
+        if z % run == run - 1:
+            ends_ref[z // run * wide:(z // run + 1) * wide, :] = lead
     norm = jnp.zeros_like(fade)
     for z in reversed(range(sections)):
+        at = slice(z * wide, (z + 1) * wide)
         decay = keep_ref[z] * fade
         norm = decay * norm + (1.0 - decay)
-        back_ref[z * wide:(z + 1) * wide, :] = 1.0 / norm
-
-
-def scan_body(turn, keep_ref, fade_ref, fore_ref, back_ref, s_ref, out_ref):
+        lead = lead * decay if (z + 1) % run else decay
+        share = 1.0 / norm
+        back_ref[at, :] = share
+        back_lead_ref[at, :] = lead * share
+
+
+def scan_body(
+    turn, keep_ref, fade_ref, fore_ref, back_ref, fore_lead_ref, back_lead_ref, ends_ref,
+    s_ref, out_ref,
+):
     sections = keep_ref.shape[0]
     wide = fade_ref.shape[0]
     fade = fade_ref[...]
-    mass = jnp.zeros_like(fade)
+    run = sections // SPANS
+    zero = jnp.zeros_like(fade)
 
     def rows(z):
         return slice(z * wide, (z + 1) * wide)
 
-    for z in range(sections):
-        decay = keep_ref[z] * fade
-        mass = decay * mass + (1.0 - decay) * s_ref[rows((z - turn) % sections), :]
-        out_ref[rows((z - turn) % sections), :] = mass * fore_ref[rows(z), :]
-    mass = jnp.zeros_like(fade)
-    for z in reversed(range(sections)):
-        decay = keep_ref[z] * fade
-        at = rows((z - turn) % sections)
-        mass = decay * mass + out_ref[at, :]
-        out_ref[at, :] = mass * back_ref[rows(z), :]
+    def seat(z):
+        return rows((z - turn) % sections)
+
+    ends = [ends_ref[rows(k), :] for k in range(SPANS)]
+    mass = [zero] * SPANS
+    for i in range(run):
+        for k in range(SPANS):
+            z = k * run + i
+            decay = keep_ref[z] * fade
+            mass[k] = decay * mass[k] + (1.0 - decay) * s_ref[seat(z), :]
+            out_ref[seat(z), :] = mass[k] * fore_ref[rows(z), :]
+    carry = [zero]
+    for k in range(SPANS - 1):
+        carry.append(mass[k] + ends[k] * carry[k])
+    mass = [zero] * SPANS
+    for i in reversed(range(run)):
+        for k in range(SPANS):
+            z = k * run + i
+            decay = keep_ref[z] * fade
+            value = out_ref[seat(z), :] + fore_lead_ref[rows(z), :] * carry[k]
+            mass[k] = decay * mass[k] + value
+            out_ref[seat(z), :] = mass[k] * back_ref[rows(z), :]
+    carry = [zero] * SPANS
+    for k in reversed(range(SPANS - 1)):
+        carry[k] = mass[k + 1] + ends[k + 1] * carry[k + 1]
+    for k in range(SPANS - 1):
+        for i in range(run):
+            z = k * run + i
+            out_ref[seat(z), :] = out_ref[seat(z), :] + back_lead_ref[rows(z), :] * carry[k]
 
 
 def finish_body(e_ref, drift_ref, out_ref):
@@ -245,9 +281,14 @@
 
     half = np.arange(rows * parts // 2)
     near = np.abs(half[:, None] - half[None, :]) <= RADIUS
-    left = half < half.size // 2
     band = near.astype(BF16)
-    joint = (near & (left[:, None] != left[None, :])).astype(BF16)
+    edge = half.size // 2
+    lane = np.arange(edge)
+    source = np.tile(np.where(lane < edge // 2, lane + half.size, lane + edge), 2)
+    target = half + edge
+    joint = np.abs(source[:, None] - target[None, :]) <= RADIUS
+    joint = joint & ((source < half.size)[:, None] != (target < half.size)[None, :])
+    joint = joint.astype(BF16)
     smoothed, rest, life = call(
         lambda *refs: smooth_body(wide, turn, *refs),
         "smooth",
@@ -264,11 +305,14 @@
         return flat.reshape(padded, LANES)
 
     long = shape(padded, LANES)
-    fade, fore, back = call(
-        norms_body, "norms", (shape(wide, LANES), long, long), [SM, VM]
+    tables = call(
+        norms_body,
+        "norms",
+        (shape(wide, LANES), long, long, long, long, shape(SPANS * wide, LANES)),
+        [SM, VM],
     )(keep, life)
-    drift = call(lambda *refs: scan_body(turn, *refs), "scan", long, [SM] + [VM] * 4)(
-        keep, fade, fore, back, swap(smoothed)
+    drift = call(lambda *refs: scan_body(turn, *refs), "scan", long, [SM] + [VM] * 7)(
+        keep, *tables, swap(smoothed)
     )
     out = call(finish_body, "finish", shape(share, rows * parts), [VM] * 2)(rest, swap(drift))
     return out.T[None]

time: 73.1 us -> 72.8 us (level)
  no operation moved by 1% of the time
where the time goes in v7:
time: 72.8 us; the launch traced here: 71.9 us
  blocking collectives  44.2 us (61%)
  starting transfers between devices  17 us (23%)
  Pallas kernels  6.07 us (8%)
  waiting for transfers between devices  3.94 us (5%)
    all_to_all x1, blocking collectives, shards(): lax.all_to_all(sent, 'ta', 0, 0, tiled=True, axis_index_groups=[ring])  24.4 us
    all_to_all x1, blocking collectives, swap(): lax.all_to_all(flat, 'gz', 0, 0, tiled=True, axis_index_groups=[order])  19.8 us
    all_to_all x1, starting transfers between devices, swap(): lax.all_to_all(flat, 'gz', 0, 0, tiled=True, axis_index_groups=[order])  17 us
    all_to_all x1, waiting for transfers between devices, swap(): lax.all_to_all(flat, 'gz', 0, 0, tiled=True, axis_index_groups=[order])  3.94 us
    pallas_call x1, Pallas kernels, shards(): call(lambda *refs: smooth_body(wide, turn, *refs), 'smooth', (shape(padde...  2.55 us
  transfers between devices with their start and end apart: 1, of which 1 were waited for; matrix products, arithmetic and copies ran while one was open for 0% of the time, Pallas kernels for 1%

profile of v7, /device:TPU:1, one launch (start us, length us, event | category | flops | bytes accessed | tf_op | source)
XLA Modules:
  0.0 71.9 jit_solution(15830518807472169848)
XLA Ops:
  0.0 1.3 %prepare.1 = f32[8,184,128]{2,1,0:T(8,128)S(1)} custom-call(f32[64,512]{1,0:T(8,128)} %bitcast.13, s32[64,512]{1,0:T(8,128)} %bitcast.14, s32[64,512]{1,0:T(8,128)} %bitcast.15, f32[64,512]{1,0:T(8,128)} %refs_3_.1), custom_call_target="tpu_custom_call" | custom-call | tf_op jit(solution)/shard_map/prepare/pallas_call | solution.py:270
  1.3 0.0 copy-start
  1.3 0.0 copy-start.1
  1.3 24.4 %all_to_all.23.refs_0_ = f32[8,184,128]{2,1,0:T(8,128)S(1)} all-to-all(f32[8,184,128]{2,1,0:T(8,128)S(1)} %prepare.1), channel_id=1, replica_groups={{7,0,1,2,3,4,5,6},{15,8,9,10,11,12,13,14},{23,16,17,18,19,20,21,22},{31..., dimensions={0} | all-to-all | bytes 1507328 | tf_op jit(solution)/shard_map/all_to_all | solution.py:280
  25.7 0.0 copy-done
  25.7 0.0 copy-done.1
  25.7 2.5 %smooth.1 = (f32[288,128]{1,0:T(8,128)}, f32[256,128]{1,0:T(8,128)S(1)}, f32[3,128]{1,0:T(4,128)S(1)}) custom-call(f32[8,184,128]{2,1,0:T(8,128)S(1)} %all_to_all.23.refs_0_, bf16[256,256]{1,0:T(8,128)(2,1)S(1)} %copy-done.1, bf16[256,256]{1,0:T(8,128)(2,1)S(1)} %copy-done), custom_call_target="tpu_custom_call" | custom-call | tf_op jit(solution)/shard_map/smooth/pallas_call | solution.py:292
  28.2 17.0 %all-to-all-start.1 = ((f32[96,384,1]{1,2,0:T(1,128)}), f32[96,384,1]{1,2,0:T(1,128)S(1)}, u32[]{:S(2)}, u32[]{:S(2)}) async-start(f32[96,384,1]{1,2,0:T(1,128)} %bitcast.3), calls=%async_computation.1 | async-start | bytes 294912 | tf_op jit(solution)/shard_map/all_to_all | solution.py:304
  45.2 0.0 copy-start.2
  45.2 0.6 copy-done.2
  45.9 0.8 %norms.1 = (f32[3,128]{1,0:T(4,128)S(1)}, f32[288,128]{1,0:T(8,128)S(1)}, f32[288,128]{1,0:T(8,128)S(1)}, f32[288,128]{1,0:T(8,128)S(1)}, f32[288,128]{1,0:T(8,128)S(1)}, /*index=5*/f32[12,128]{1,0:T(8,128)S(1)}) custom-call(f32[96]{0:T(128)S(1)} %copy-done.2, f32[3,128]{1,0:T(4,128)S(1)} %get-tuple-element.15.life_ref), custom_call_target="tpu_custom_call" | custom-call | tf_op jit(solution)/shard_map/norms/pallas_call | solution.py:308
  46.7 3.9 %all-to-all-done.1 = f32[96,384,1]{1,2,0:T(1,128)S(1)} async-done(((f32[96,384,1]{1,2,0:T(1,128)}), f32[96,384,1]{1,2,0:T(1,128)S(1)}, u32[]{:S(2)}, u32[]{:S(2)}) %all-to-all-start.1) | async-done | bytes 147488 | tf_op jit(solution)/shard_map/all_to_all | solution.py:304
  50.7 0.8 %scan.1 = f32[288,128]{1,0:T(8,128)S(1)} custom-call(f32[96]{0:T(128)S(1)} %copy-done.2, f32[3,128]{1,0:T(4,128)S(1)} %get-tuple-element.16.refs_1_, f32[288,128]{1,0:T(8,128)S(1)} %get-tuple-element.17.refs_2_, f32[288,128]{1,0:T(8,128)S(1)} %get-tuple-element.18.refs_3_, f32[288,128]{1,0:T(8,128)S(1)} %get-tuple-element.19.refs_4_, ...), custom_call_target="tpu_custom_call" | custom-call | tf_op jit(solution)/shard_map/scan/pallas_call | solution.py:314
  51.4 19.8 %all_to_all.24 = f32[96,384,1]{1,2,0:T(1,128)S(1)} all-to-all(f32[96,384,1]{1,2,0:T(1,128)S(1)} %bitcast.12), channel_id=1, replica_groups={{536,544,552,560,568,576,584,592,600,608,616,624,632,640,648,656,664,67..., dimensions={0} | all-to-all | bytes 294912 | tf_op jit(solution)/shard_map/all_to_all | solution.py:304
  71.2 0.7 finish.1
Async XLA Ops:
  1.3 24.4 %copy-start = (bf16[256,256]{1,0:T(8,128)(2,1)S(1)}, bf16[256,256]{1,0:T(8,128)(2,1)}, u32[]{:S(2)}) copy-start(bf16[256,256]{1,0:T(8,128)(2,1)} %constant.5.clone.refs_2_) | copy-start | bytes 393220
  1.3 24.4 %copy-start.1 = (bf16[256,256]{1,0:T(8,128)(2,1)S(1)}, bf16[256,256]{1,0:T(8,128)(2,1)}, u32[]{:S(2)}) copy-start(bf16[256,256]{1,0:T(8,128)(2,1)} %constant.4.clone.refs_1_) | copy-start | bytes 393220
  28.2 22.4 %all-to-all-start.1 = ((f32[96,384,1]{1,2,0:T(1,128)}), f32[96,384,1]{1,2,0:T(1,128)S(1)}, u32[]{:S(2)}, u32[]{:S(2)}) async-start(f32[96,384,1]{1,2,0:T(1,128)} %bitcast.3), calls=%async_computation.1 | async-start | bytes 294912 | tf_op jit(solution)/shard_map/all_to_all | solution.py:304
  45.2 0.7 copy-start.2

commit v8 on v7

--- a/solution.py
+++ b/solution.py
@@ -12,6 +12,7 @@
 START = 67
 FIRST = 7
 SPANS = 4
+DEPTH = 12
 LANES = 128
 F32 = jnp.float32
 BF16 = jnp.bfloat16
@@ -19,6 +20,12 @@
 HB = pl.BlockSpec(memory_space=pltpu.HBM)
 SM = pl.BlockSpec(memory_space=pltpu.SMEM)
 PARAMS = pltpu.CompilerParams(vmem_limit_bytes=16 << 20)
+
+
+def seat_of(g, turn, sections):
+    high = sections // DEPTH
+    level = (g % DEPTH + DEPTH - turn % DEPTH) % DEPTH
+    return level * high + (g // DEPTH + high - turn // DEPTH) % high
 
 
 def prepare_body(
@@ -46,7 +53,7 @@
     for c in range(0, cols, LANES):
         both_ref[HALO + c:HALO + c + LANES, :] = both[:, c:c + LANES].T
     sections = lax.axis_size("gz")
-    first = lax.rem(lax.axis_index("gz") + sections - turn, sections) * wide
+    first = seat_of(lax.axis_index("gz"), turn, sections) * wide
     for t in range(parts):
         slot = (t - FIRST) % parts
         out_ref[slot, :span, :] = both_ref[share * t:share * t + span, :]
@@ -120,7 +127,7 @@
     field = jnp.concatenate(fields, axis=1)
 
     sections = lax.axis_size("gz")
-    first = lax.rem(lax.axis_index("gz") + sections - turn, sections) * wide
+    first = seat_of(lax.axis_index("gz"), turn, sections) * wide
     left = lax.broadcasted_iota(jnp.int32, (1, LANES), 1) < half
     for i in range(wide):
         pair = 2 * jnp.minimum((first + i) // share, parts // 2 - 1)
@@ -199,7 +206,7 @@
         return slice(z * wide, (z + 1) * wide)
 
     def seat(z):
-        return rows((z - turn) % sections)
+        return rows(seat_of(z, turn, sections))
 
     ends = [ends_ref[rows(k), :] for k in range(SPANS)]
     mass = [zero] * SPANS
@@ -297,7 +304,9 @@
         [pltpu.VMEM((total - 2 * RADIUS, rows * parts), F32)] * 2,
     )(sent, band, joint)
 
-    order = [(i + turn) % sections for i in range(sections)]
+    order = [0] * sections
+    for g in range(sections):
+        order[seat_of(g, turn, sections)] = g
 
     def swap(values):
         flat = values.reshape(padded * LANES)

time: 72.8 us -> 72.5 us (level)
  blocking collectives: 44.2 us -> 43.4 us
    all_to_all x1, blocking collectives: 19.8 us -> 19 us  [swap(): lax.all_to_all(flat, 'gz', 0, 0, tiled=True, axis_index_groups=[order])]
where the time goes in v8:
time: 72.5 us; the launch traced here: 71.6 us
  blocking collectives  43.4 us (60%)
  starting transfers between devices  17.1 us (24%)
  Pallas kernels  6.06 us (8%)
  waiting for transfers between devices  4.28 us (6%)
    all_to_all x1, blocking collectives, shards(): lax.all_to_all(sent, 'ta', 0, 0, tiled=True, axis_index_groups=[ring])  24.4 us
    all_to_all x1, blocking collectives, swap(): lax.all_to_all(flat, 'gz', 0, 0, tiled=True, axis_index_groups=[order])  19 us
    all_to_all x1, starting transfers between devices, swap(): lax.all_to_all(flat, 'gz', 0, 0, tiled=True, axis_index_groups=[order])  17.1 us
    all_to_all x1, waiting for transfers between devices, swap(): lax.all_to_all(flat, 'gz', 0, 0, tiled=True, axis_index_groups=[order])  4.28 us
    pallas_call x1, Pallas kernels, shards(): call(lambda *refs: smooth_body(wide, turn, *refs), 'smooth', (shape(padde...  2.55 us
  transfers between devices with their start and end apart: 1, of which 1 were waited for; matrix products, arithmetic and copies ran while one was open for 0% of the time, Pallas kernels for 1%

profile of v8, /device:TPU:1, one launch (start us, length us, event | category | flops | bytes accessed | tf_op | source)
XLA Modules:
  0.0 71.6 jit_solution(10216468228349373052)
XLA Ops:
  0.0 1.3 %prepare.1 = f32[8,184,128]{2,1,0:T(8,128)S(1)} custom-call(f32[64,512]{1,0:T(8,128)} %bitcast.13, s32[64,512]{1,0:T(8,128)} %bitcast.14, s32[64,512]{1,0:T(8,128)} %bitcast.15, f32[64,512]{1,0:T(8,128)} %refs_3_.1), custom_call_target="tpu_custom_call" | custom-call | tf_op jit(solution)/shard_map/prepare/pallas_call | solution.py:277
  1.3 0.0 copy-start
  1.3 0.0 copy-start.1
  1.3 24.4 %all_to_all.23.refs_0_ = f32[8,184,128]{2,1,0:T(8,128)S(1)} all-to-all(f32[8,184,128]{2,1,0:T(8,128)S(1)} %prepare.1), channel_id=1, replica_groups={{7,0,1,2,3,4,5,6},{15,8,9,10,11,12,13,14},{23,16,17,18,19,20,21,22},{31..., dimensions={0} | all-to-all | bytes 1507328 | tf_op jit(solution)/shard_map/all_to_all | solution.py:287
  25.7 0.0 copy-done
  25.7 0.0 copy-done.1
  25.7 2.5 %smooth.1 = (f32[288,128]{1,0:T(8,128)}, f32[256,128]{1,0:T(8,128)S(1)}, f32[3,128]{1,0:T(4,128)S(1)}) custom-call(f32[8,184,128]{2,1,0:T(8,128)S(1)} %all_to_all.23.refs_0_, bf16[256,256]{1,0:T(8,128)(2,1)S(1)} %copy-done.1, bf16[256,256]{1,0:T(8,128)(2,1)S(1)} %copy-done), custom_call_target="tpu_custom_call" | custom-call | tf_op jit(solution)/shard_map/smooth/pallas_call | solution.py:299
  28.2 17.1 %all-to-all-start.1 = ((f32[96,384,1]{1,2,0:T(1,128)}), f32[96,384,1]{1,2,0:T(1,128)S(1)}, u32[]{:S(2)}, u32[]{:S(2)}) async-start(f32[96,384,1]{1,2,0:T(1,128)} %bitcast.3), calls=%async_computation.1 | async-start | bytes 294912 | tf_op jit(solution)/shard_map/all_to_all | solution.py:313
  45.3 0.0 copy-start.2
  45.3 0.6 copy-done.2
  46.0 0.8 %norms.1 = (f32[3,128]{1,0:T(4,128)S(1)}, f32[288,128]{1,0:T(8,128)S(1)}, f32[288,128]{1,0:T(8,128)S(1)}, f32[288,128]{1,0:T(8,128)S(1)}, f32[288,128]{1,0:T(8,128)S(1)}, /*index=5*/f32[12,128]{1,0:T(8,128)S(1)}) custom-call(f32[96]{0:T(128)S(1)} %copy-done.2, f32[3,128]{1,0:T(4,128)S(1)} %get-tuple-element.15.life_ref), custom_call_target="tpu_custom_call" | custom-call | tf_op jit(solution)/shard_map/norms/pallas_call | solution.py:317
  46.8 4.3 %all-to-all-done.1 = f32[96,384,1]{1,2,0:T(1,128)S(1)} async-done(((f32[96,384,1]{1,2,0:T(1,128)}), f32[96,384,1]{1,2,0:T(1,128)S(1)}, u32[]{:S(2)}, u32[]{:S(2)}) %all-to-all-start.1) | async-done | bytes 147488 | tf_op jit(solution)/shard_map/all_to_all | solution.py:313
  51.1 0.8 %scan.1 = f32[288,128]{1,0:T(8,128)S(1)} custom-call(f32[96]{0:T(128)S(1)} %copy-done.2, f32[3,128]{1,0:T(4,128)S(1)} %get-tuple-element.16.refs_1_, f32[288,128]{1,0:T(8,128)S(1)} %get-tuple-element.17.refs_2_, f32[288,128]{1,0:T(8,128)S(1)} %get-tuple-element.18.refs_3_, f32[288,128]{1,0:T(8,128)S(1)} %get-tuple-element.19.refs_4_, ...), custom_call_target="tpu_custom_call" | custom-call | tf_op jit(solution)/shard_map/scan/pallas_call | solution.py:323
  51.9 19.0 %all_to_all.24 = f32[96,384,1]{1,2,0:T(1,128)S(1)} all-to-all(f32[96,384,1]{1,2,0:T(1,128)S(1)} %bitcast.12), channel_id=1, replica_groups={{536,632,728,56,152,248,344,440,544,640,736,64,160,256,352,448,552,648,..., dimensions={0} | all-to-all | bytes 294912 | tf_op jit(solution)/shard_map/all_to_all | solution.py:313
  70.9 0.7 finish.1
Async XLA Ops:
  1.3 24.4 %copy-start = (bf16[256,256]{1,0:T(8,128)(2,1)S(1)}, bf16[256,256]{1,0:T(8,128)(2,1)}, u32[]{:S(2)}) copy-start(bf16[256,256]{1,0:T(8,128)(2,1)} %constant.5.clone.refs_2_) | copy-start | bytes 393220
  1.3 24.4 %copy-start.1 = (bf16[256,256]{1,0:T(8,128)(2,1)S(1)}, bf16[256,256]{1,0:T(8,128)(2,1)}, u32[]{:S(2)}) copy-start(bf16[256,256]{1,0:T(8,128)(2,1)} %constant.4.clone.refs_1_) | copy-start | bytes 393220
  28.2 22.9 %all-to-all-start.1 = ((f32[96,384,1]{1,2,0:T(1,128)}), f32[96,384,1]{1,2,0:T(1,128)S(1)}, u32[]{:S(2)}, u32[]{:S(2)}) async-start(f32[96,384,1]{1,2,0:T(1,128)} %bitcast.3), calls=%async_computation.1 | async-start | bytes 294912 | tf_op jit(solution)/shard_map/all_to_all | solution.py:313
  45.3 0.7 copy-start.2

commit v9 on v8

--- a/solution.py
+++ b/solution.py
@@ -55,7 +55,7 @@
     sections = lax.axis_size("gz")
     first = seat_of(lax.axis_index("gz"), turn, sections) * wide
     for t in range(parts):
-        slot = (t - FIRST) % parts
+        slot = (FIRST - t) % parts
         out_ref[slot, :span, :] = both_ref[share * t:share * t + span, :]
         out_ref[slot, span:, :] = jnp.zeros((depth - span, LANES), F32)
         for i in range(wide):
@@ -119,8 +119,8 @@
     left = lax.broadcasted_iota(jnp.int32, (total, LANES), 1) < half
     weights, fields = [], []
     for t in range(0, parts, 2):
-        a = in_ref[(t - FIRST) % parts, :total, :]
-        b = in_ref[(t + 1 - FIRST) % parts, :total, :]
+        a = in_ref[(FIRST - t) % parts, :total, :]
+        b = in_ref[(FIRST - t - 1) % parts, :total, :]
         weights.append(jnp.where(left, a, pltpu.roll(b, half, 1)))
         fields.append(jnp.where(left, pltpu.roll(a, half, 1), b))
     weight = jnp.concatenate(weights, axis=1)
@@ -131,9 +131,9 @@
     left = lax.broadcasted_iota(jnp.int32, (1, LANES), 1) < half
     for i in range(wide):
         pair = 2 * jnp.minimum((first + i) // share, parts // 2 - 1)
-        shift = parts - FIRST
-        a = in_ref[lax.rem(pair + shift, parts), total + i:total + i + 1, :]
-        b = in_ref[lax.rem(pair + 1 + shift, parts), total + i:total + i + 1, :]
+        shift = parts + FIRST
+        a = in_ref[lax.rem(shift - pair, parts), total + i:total + i + 1, :]
+        b = in_ref[lax.rem(shift - pair - 1, parts), total + i:total + i + 1, :]
         life_ref[i:i + 1, :] = jnp.where(left, a, b)
 
     band = band_ref[...]
@@ -283,7 +283,7 @@
         + [pltpu.VMEM((cols + 2 * HALO, LANES), F32), pltpu.VMEM((cols, LANES), F32)]
         + [pltpu.SemaphoreType.DMA((4,))],
     )(*(in_hbm(a) for a in (log_mean[0], tile_mask[0], coverage[0], lifetime)))
-    ring = [(i + FIRST) % parts for i in range(parts)]
+    ring = [(FIRST - i) % parts for i in range(parts)]
     sent = lax.all_to_all(sent, "ta", 0, 0, tiled=True, axis_index_groups=[ring])
 
     half = np.arange(rows * parts // 2)

time: 72.5 us -> 72.5 us (level)
  waiting for transfers between devices: 4.28 us -> 3.5 us
    all_to_all x1, waiting for transfers between devices: 4.28 us -> 3.5 us  [swap(): lax.all_to_all(flat, 'gz', 0, 0, tiled=True, axis_index_groups=[order])]
where the time goes in v9:
time: 72.5 us; the launch traced here: 71 us
  blocking collectives  43.7 us (60%)
  starting transfers between devices  17.1 us (24%)
  Pallas kernels  6.06 us (8%)
  waiting for transfers between devices  3.5 us (5%)
    all_to_all x1, blocking collectives, shards(): lax.all_to_all(sent, 'ta', 0, 0, tiled=True, axis_index_groups=[ring])  24.1 us
    all_to_all x1, blocking collectives, swap(): lax.all_to_all(flat, 'gz', 0, 0, tiled=True, axis_index_groups=[order])  19.6 us
    all_to_all x1, starting transfers between devices, swap(): lax.all_to_all(flat, 'gz', 0, 0, tiled=True, axis_index_groups=[order])  17.1 us
    all_to_all x1, waiting for transfers between devices, swap(): lax.all_to_all(flat, 'gz', 0, 0, tiled=True, axis_index_groups=[order])  3.5 us
    pallas_call x1, Pallas kernels, shards(): call(lambda *refs: smooth_body(wide, turn, *refs), 'smooth', (shape(padde...  2.55 us
  transfers between devices with their start and end apart: 1, of which 1 were waited for; matrix products, arithmetic and copies ran while one was open for 0% of the time, Pallas kernels for 1%

profile of v9, /device:TPU:1, one launch (start us, length us, event | category | flops | bytes accessed | tf_op | source)
XLA Modules:
  0.0 71.0 jit_solution(345039453896875601)
XLA Ops:
  0.0 1.3 %prepare.1 = f32[8,184,128]{2,1,0:T(8,128)S(1)} custom-call(f32[64,512]{1,0:T(8,128)} %bitcast.13, s32[64,512]{1,0:T(8,128)} %bitcast.14, s32[64,512]{1,0:T(8,128)} %bitcast.15, f32[64,512]{1,0:T(8,128)} %refs_3_.1), custom_call_target="tpu_custom_call" | custom-call | tf_op jit(solution)/shard_map/prepare/pallas_call | solution.py:277
  1.3 0.0 copy-start
  1.3 0.0 copy-start.1
  1.3 24.1 %all_to_all.23.refs_0_ = f32[8,184,128]{2,1,0:T(8,128)S(1)} all-to-all(f32[8,184,128]{2,1,0:T(8,128)S(1)} %prepare.1), channel_id=1, replica_groups={{7,6,5,4,3,2,1,0},{15,14,13,12,11,10,9,8},{23,22,21,20,19,18,17,16},{31..., dimensions={0} | all-to-all | bytes 1507328 | tf_op jit(solution)/shard_map/all_to_all | solution.py:287
  25.4 0.0 copy-done
  25.4 0.0 copy-done.1
  25.4 2.5 %smooth.1 = (f32[288,128]{1,0:T(8,128)}, f32[256,128]{1,0:T(8,128)S(1)}, f32[3,128]{1,0:T(4,128)S(1)}) custom-call(f32[8,184,128]{2,1,0:T(8,128)S(1)} %all_to_all.23.refs_0_, bf16[256,256]{1,0:T(8,128)(2,1)S(1)} %copy-done.1, bf16[256,256]{1,0:T(8,128)(2,1)S(1)} %copy-done), custom_call_target="tpu_custom_call" | custom-call | tf_op jit(solution)/shard_map/smooth/pallas_call | solution.py:299
  27.9 17.1 %all-to-all-start.1 = ((f32[96,384,1]{1,2,0:T(1,128)}), f32[96,384,1]{1,2,0:T(1,128)S(1)}, u32[]{:S(2)}, u32[]{:S(2)}) async-start(f32[96,384,1]{1,2,0:T(1,128)} %bitcast.3), calls=%async_computation.1 | async-start | bytes 294912 | tf_op jit(solution)/shard_map/all_to_all | solution.py:313
  45.0 0.0 copy-start.2
  45.0 0.6 copy-done.2
  45.7 0.8 %norms.1 = (f32[3,128]{1,0:T(4,128)S(1)}, f32[288,128]{1,0:T(8,128)S(1)}, f32[288,128]{1,0:T(8,128)S(1)}, f32[288,128]{1,0:T(8,128)S(1)}, f32[288,128]{1,0:T(8,128)S(1)}, /*index=5*/f32[12,128]{1,0:T(8,128)S(1)}) custom-call(f32[96]{0:T(128)S(1)} %copy-done.2, f32[3,128]{1,0:T(4,128)S(1)} %get-tuple-element.15.life_ref), custom_call_target="tpu_custom_call" | custom-call | tf_op jit(solution)/shard_map/norms/pallas_call | solution.py:317
  46.5 3.5 %all-to-all-done.1 = f32[96,384,1]{1,2,0:T(1,128)S(1)} async-done(((f32[96,384,1]{1,2,0:T(1,128)}), f32[96,384,1]{1,2,0:T(1,128)S(1)}, u32[]{:S(2)}, u32[]{:S(2)}) %all-to-all-start.1) | async-done | bytes 147488 | tf_op jit(solution)/shard_map/all_to_all | solution.py:313
  50.0 0.8 %scan.1 = f32[288,128]{1,0:T(8,128)S(1)} custom-call(f32[96]{0:T(128)S(1)} %copy-done.2, f32[3,128]{1,0:T(4,128)S(1)} %get-tuple-element.16.refs_1_, f32[288,128]{1,0:T(8,128)S(1)} %get-tuple-element.17.refs_2_, f32[288,128]{1,0:T(8,128)S(1)} %get-tuple-element.18.refs_3_, f32[288,128]{1,0:T(8,128)S(1)} %get-tuple-element.19.refs_4_, ...), custom_call_target="tpu_custom_call" | custom-call | tf_op jit(solution)/shard_map/scan/pallas_call | solution.py:323
  50.8 19.6 %all_to_all.24 = f32[96,384,1]{1,2,0:T(1,128)S(1)} all-to-all(f32[96,384,1]{1,2,0:T(1,128)S(1)} %bitcast.12), channel_id=1, replica_groups={{536,632,728,56,152,248,344,440,544,640,736,64,160,256,352,448,552,648,..., dimensions={0} | all-to-all | bytes 294912 | tf_op jit(solution)/shard_map/all_to_all | solution.py:313
  70.4 0.7 finish.1
Async XLA Ops:
  1.3 24.1 %copy-start = (bf16[256,256]{1,0:T(8,128)(2,1)S(1)}, bf16[256,256]{1,0:T(8,128)(2,1)}, u32[]{:S(2)}) copy-start(bf16[256,256]{1,0:T(8,128)(2,1)} %constant.5.clone.refs_2_) | copy-start | bytes 393220
  1.3 24.1 %copy-start.1 = (bf16[256,256]{1,0:T(8,128)(2,1)S(1)}, bf16[256,256]{1,0:T(8,128)(2,1)}, u32[]{:S(2)}) copy-start(bf16[256,256]{1,0:T(8,128)(2,1)} %constant.4.clone.refs_1_) | copy-start | bytes 393220
  27.9 22.1 %all-to-all-start.1 = ((f32[96,384,1]{1,2,0:T(1,128)}), f32[96,384,1]{1,2,0:T(1,128)S(1)}, u32[]{:S(2)}, u32[]{:S(2)}) async-start(f32[96,384,1]{1,2,0:T(1,128)} %bitcast.3), calls=%async_computation.1 | async-start | bytes 294912 | tf_op jit(solution)/shard_map/all_to_all | solution.py:313
  45.0 0.7 copy-start.2
